TPU v7x, 32 devices: a whole 2x2x4 slice. The times are simulated.
32 devices in a mesh: groups: 2 (over y), gx: 4 (over z), gy: 2 (over x), gz: 2 (over core).
Axes of the slice: x: 2, y: 2, z: 4, core: 2. Of those that a mesh axis runs over, the one named last changes fastest.
Arguments:
- heat: float32 [64, 256, 256], P('gz', ('groups', 'gx'), 'gy'), parts along dimension 1, may hold values from -6 to 6
- material: int32 [64, 256, 256], P('gz', ('groups', 'gx'), 'gy'), parts along dimension 1, may hold values from 0 to 7
- table: float32 [8], replicated, may hold values from 0.5 to 8
Outputs:
- temperature: float32 [64, 256, 256], P('gz', ('groups', 'gx'), 'gy'), parts along dimension 1
There are 2 independent parts, one for each index of `groups`. A program takes and returns all parts, laid end to end along the dimension named above; an argument that names none is the same for every part. Nothing has to cross between parts.
All inputs are finite; a program needn't handle non-finite values.
Results may differ from a plain program's by a relative error of at most 0.0003.
Values sent between devices are 32-bit elements; how exact they have to be, the bound alone decides.
A program may use at most 64 MiB of HBM per device.

v0:
```python
import math

import jax
import jax.numpy as jnp
from jax import lax
from jax.sharding import PartitionSpec as P

BLOCK = 16
PRE = 2
POST = 2


def padded_2(block, sides, width):
    for axis, dim in sides:
        count = lax.axis_size(axis)
        forward = [(i, i + 1) for i in range(count - 1)]
        backward = [(target, source) for source, target in forward]
        low = lax.ppermute(
            lax.slice_in_dim(block, block.shape[dim] - width, None, axis=dim), axis, forward
        )
        high = lax.ppermute(lax.slice_in_dim(block, 0, width, axis=dim), axis, backward)
        block = jnp.concatenate([low, block, high], axis=dim)
    return block


def harmonic(center, other):
    inside = other > 0.0
    total = jnp.where(inside, center + other, 1.0)
    return jnp.where(inside, 2.0 * center * other / total, center)


def shifted(padded, dim, step, shape, margin):
    start = [margin, margin, margin]
    start[dim] = start[dim] + step
    return padded[
        start[0] : start[0] + shape[0],
        start[1] : start[1] + shape[1],
        start[2] : start[2] + shape[2],
    ]


def stencil_weights(kpad, shape, margin):
    center = shifted(kpad, 0, 0, shape, margin)
    weights = []
    for dim in range(3):
        for step in (-1, 1):
            weights.append(harmonic(center, shifted(kpad, dim, step, shape, margin)))
    return weights


def neighbour_sum(weights, upad, shape, margin):
    total = None
    index = 0
    for dim in range(3):
        for step in (-1, 1):
            term = weights[index] * shifted(upad, dim, step, shape, margin)
            total = term if total is None else total + term
            index = index + 1
    return total


def weight_total(weights):
    return weights[0] + weights[1] + weights[2] + weights[3] + weights[4] + weights[5]


def parity_of(shape):
    return (
        lax.broadcasted_iota(jnp.int32, shape, 0)
        + lax.broadcasted_iota(jnp.int32, shape, 1)
        + lax.broadcasted_iota(jnp.int32, shape, 2)
    ) % 2


def sine_table(count):
    idx = jnp.arange(1, count + 1).astype(jnp.float32)
    return jnp.sin(math.pi * idx[:, None] * idx[None, :] / (count + 1))


def eigen_of(position, count):
    return 2.0 - 2.0 * jnp.cos(math.pi * (position + 1).astype(jnp.float32) / (count + 1))


def coarse_block(block, kbar):
    high = lax.Precision.HIGHEST
    lay_z, lay_x, lay_y = block.shape
    count_x, count_y, count_z = (lax.axis_size("gx"), lax.axis_size("gy"), lax.axis_size("gz"))
    full_z, full_x, full_y = (lay_z * count_z, lay_x * count_x, lay_y * count_y)
    scale = BLOCK * BLOCK * 8.0 / ((full_z + 1) * (full_x + 1) * (full_y + 1) * kbar)
    table_z, table_x, table_y = (sine_table(full_z), sine_table(full_x), sine_table(full_y))
    piece = block.transpose(1, 0, 2)[None]
    column = lax.all_gather(piece, ("gy", "gz"), axis=0, tiled=True)
    column = column.reshape(count_y, count_z, lay_x, lay_z, lay_y)
    column = column.transpose(2, 1, 3, 0, 4).reshape(lay_x, full_z, full_y)
    hat = jnp.einsum("az,xzy->xay", table_z, column, precision=high)
    hat = jnp.einsum("by,xay->xab", table_y, hat, precision=high)
    hat = hat.reshape(lay_x, full_z * full_y)
    turned = lax.all_to_all(hat, "gx", split_axis=1, concat_axis=0, tiled=True)
    rows_here = turned.shape[1]
    flat = lax.axis_index("gx") * rows_here + jnp.arange(rows_here)
    lam_zy = eigen_of(flat // full_y, full_z) + eigen_of(flat % full_y, full_y)
    turned = jnp.einsum("bx,xr->br", table_x, turned, precision=high)
    turned = turned / (eigen_of(jnp.arange(full_x), full_x)[:, None] + lam_zy[None, :])
    turned = jnp.einsum("bx,xr->br", table_x, turned, precision=high)
    back = lax.all_to_all(turned, "gx", split_axis=0, concat_axis=1, tiled=True)
    back = back.reshape(lay_x, full_z, full_y)
    back = jnp.einsum("az,xzy->xay", table_z, back, precision=high)
    back = jnp.einsum("by,xay->xab", table_y, back, precision=high) * scale
    start_z = lax.axis_index("gz") * lay_z
    start_y = lax.axis_index("gy") * lay_y
    mine = lax.dynamic_slice(back, (jnp.int32(0), start_z, start_y), (lay_x, lay_z, lay_y))
    return mine.transpose(1, 0, 2)


def per_device(heat, material, table):
    shape = heat.shape
    kappa = jnp.zeros(shape, jnp.float32)
    for mat in range(table.shape[0]):
        kappa = kappa + jnp.where(material == mat, table[mat], 0.0)
    parity = parity_of(shape)
    red = parity == 0
    black = parity == 1
    kpad = padded_2(kappa, (("gx", 1), ("gy", 2), ("gz", 0)), 1)
    weights = stencil_weights(kpad, shape, 1)
    diag = weight_total(weights)

    def sweep(field):
        for mask in (red, black):
            upad = padded_2(field, (("gx", 1), ("gy", 2), ("gz", 0)), 1)
            field = jnp.where(mask, (heat + neighbour_sum(weights, upad, shape, 1)) / diag, field)
        return field

    field = jnp.zeros(shape, jnp.float32)
    for turn in range(PRE):
        field = sweep(field)
    upad = padded_2(field, (("gx", 1), ("gy", 2), ("gz", 0)), 1)
    residual = heat - (diag * field - neighbour_sum(weights, upad, shape, 1))
    lay_z, lay_x, lay_y = (shape[0] // BLOCK, shape[1] // BLOCK, shape[2] // BLOCK)
    block = residual.reshape(lay_z, BLOCK, lay_x, BLOCK, lay_y, BLOCK).mean(axis=(1, 3, 5))
    correction = coarse_block(block, jnp.mean(table))
    fine = jnp.broadcast_to(
        correction[:, None, :, None, :, None], (lay_z, BLOCK, lay_x, BLOCK, lay_y, BLOCK)
    ).reshape(shape)
    field = field + fine
    for turn in range(POST):
        field = sweep(field)
    return field


def solution(mesh):
    in_specs = (P("gz", ("groups", "gx"), "gy"), P("gz", ("groups", "gx"), "gy"), P())
    out_specs = P("gz", ("groups", "gx"), "gy")
    return jax.shard_map(
        per_device, mesh=mesh, in_specs=in_specs, out_specs=out_specs, check_vma=False
    )
```

profile of v0, /device:TPU:0, one launch (start us, length us, event | category | flops | bytes accessed | tf_op | source)
XLA Modules:
  0.0 355.7 jit_solution(12026305665674574248)
XLA Ops:
  1.6 6.5 %select_add_fusion = f32[32,32,128]{2,1,0:T(8,128)S(1)} fusion(s32[32,32,128]{2,1,0:T(8,128)} %param.4, f32[]{:T(128)} %bitcast.7, f32[]{:T(128)} %bitcast.6, f32[]{:T(128)} %bitcast.5, f32[]{:T(128)} %bitcast.4, f32[]{:T(128)} %bitcast.3, f32[]{:T(128)} %bitcast.2, f32[]{:T(128)} %bitcast.1, f32[]{:T(128)} %bitcast), kind=kLoop, calls=%fused_computation.339 | loop fusion | flops 3014656 | bytes 1048608 | tf_op jit(solution)/shard_map/add | solution.py:118
  8.2 4.9 %collective-permute-start = (f32[32,1,128]{2,1,0:T(1,128)S(1)}, f32[32,1,128]{2,1,0:T(1,128)S(1)}, u32[]{:S(2)}, u32[]{:S(2)}) collective-permute-start(f32[32,1,128]{2,1,0:T(1,128)S(1)} %get-tuple-element.67), channel_id=1, source_target_pairs={{0,4},{4,8},{8,12},{1,5},{5,9},{9,13},{2,6},{6,10},{10,14},{3,7},{... | collective-permute-start | bytes 49160 | tf_op jit(solution)/shard_map/ppermute | solution.py:18
  14.5 4.5 %collective-permute-start.5 = (f32[32,1,128]{2,1,0:T(1,128)S(1)}, f32[32,1,128]{2,1,0:T(1,128)S(1)}, u32[]{:S(2)}, u32[]{:S(2)}) collective-permute-start(f32[32,1,128]{2,1,0:T(1,128)S(1)} %broadcast.221), channel_id=1, source_target_pairs={{0,4},{4,8},{8,12},{1,5},{5,9},{9,13},{2,6},{6,10},{10,14},{3,7},{... | collective-permute-start | bytes 49160 | tf_op jit(solution)/shard_map/ppermute | solution.py:18
  21.0 3.4 collective-permute-start.2
  28.7 4.5 %collective-permute-start.7 = (f32[32,34,1]{1,0,2:T(8,128)S(1)}, f32[32,34,1]{1,0,2:T(8,128)S(1)}, u32[]{:S(2)}, u32[]{:S(2)}) collective-permute-start(f32[32,34,1]{1,0,2:T(8,128)S(1)} %copy.98), channel_id=1, source_target_pairs={{0,2},{1,3},{4,6},{5,7},{8,10},{9,11},{12,14},{13,15},{16,18},{17,... | collective-permute-start | bytes 13064 | tf_op jit(solution)/shard_map/ppermute | solution.py:18
  48.5 7.3 %fusion.7 = (f32[32,32,128]{2,1,0:T(8,128)S(1)}, f32[32,32,128]{2,1,0:T(8,128)S(1)}, f32[32,32,128]{2,1,0:T(8,128)S(1)}, f32[32,32,128]{2,1,0:T(8,128)S(1)}, f32[32,32,128]{2,1,0:T(8,128)S(1)}) fusion(f32[32,32,128]{2,1,0:T(8,128)} %copy-done.9, f32[32,32,128]{2,1,0:T(8,128)S(1)} %copy-done, f32[32,1,128]{2,1,0:T(1,128)S(1)} %collective-permute-done.5, ...), kind=kLoop, calls=%fused_computation.25 | loop fusion | flops 13631488 | bytes 4347968 | tf_op jit(solution)/shard_map/jit(_where)/select_n | solution.py:129
  55.9 4.5 %collective-permute-start.12 = (f32[32,1,128]{2,1,0:T(1,128)S(1)}, f32[32,1,128]{2,1,0:T(1,128)S(1)}, u32[]{:S(2)}, u32[]{:S(2)}) collective-permute-start(f32[32,1,128]{2,1,0:T(1,128)S(1)} %get-tuple-element.64), channel_id=1, source_target_pairs={{0,4},{4,8},{8,12},{1,5},{5,9},{9,13},{2,6},{6,10},{10,14},{3,7},{... | collective-permute-start | bytes 49160 | tf_op jit(solution)/shard_map/ppermute | solution.py:18
  61.9 4.2 %collective-permute-done.13 = f32[32,1,128]{2,1,0:T(1,128)S(1)} collective-permute-done((f32[32,1,128]{2,1,0:T(1,128)S(1)}, f32[32,1,128]{2,1,0:T(1,128)S(1)}, u32[]{:S(2)}, u32[]{:S(2)}) %collective-permute-start.13) | collective-permute-done | bytes 16416 | tf_op jit(solution)/shard_map/ppermute | solution.py:21
  68.8 4.5 %collective-permute-start.14 = (f32[32,34,1]{1,0,2:T(8,128)S(1)}, f32[32,34,1]{1,0,2:T(8,128)S(1)}, u32[]{:S(2)}, u32[]{:S(2)}) collective-permute-start(f32[32,34,1]{1,0,2:T(8,128)S(1)} %copy.106), channel_id=1, source_target_pairs={{0,2},{1,3},{4,6},{5,7},{8,10},{9,11},{12,14},{13,15},{16,18},{17,... | collective-permute-start | bytes 13064 | tf_op jit(solution)/shard_map/ppermute | solution.py:18
  86.9 5.5 %fusion.111 = f32[32,32,128]{2,1,0:T(8,128)S(1)} fusion(f32[32,32,128]{2,1,0:T(8,128)} %copy-done.2, f32[32,32,128]{2,1,0:T(8,128)S(1)} %copy-done, f32[32,32,128]{2,1,0:T(8,128)S(1)} %get-tuple-element.9, f32[32,34,1]{2,1,0:T(8,128)} %copy.109, f32[32,1,128]{2,1,0:T(1,128)S(1)} %collective-permute-done.13, f32[32,1,128]{2,1,0:T(1,128)S(1)} %collective-permute-done.12, ...), kind=kLoop, calls=%fused_computation.256 | loop fusion | flops 8650752 | bytes 4303904 | tf_op jit(solution)/shard_map/jit(_where)/select_n | solution.py:129
  92.4 3.5 collective-permute-start.18
  97.3 4.2 %collective-permute-done.19 = f32[32,1,128]{2,1,0:T(1,128)S(1)} collective-permute-done((f32[32,1,128]{2,1,0:T(1,128)S(1)}, f32[32,1,128]{2,1,0:T(1,128)S(1)}, u32[]{:S(2)}, u32[]{:S(2)}) %collective-permute-start.19) | collective-permute-done | bytes 16416 | tf_op jit(solution)/shard_map/ppermute | solution.py:21
  119.5 5.5 %fusion.97 = f32[32,32,128]{2,1,0:T(8,128)S(1)} fusion(f32[32,32,128]{2,1,0:T(8,128)} %copy-done.6, f32[32,32,128]{2,1,0:T(8,128)S(1)} %copy-done, f32[32,32,128]{2,1,0:T(8,128)S(1)} %get-tuple-element.9, f32[32,34,1]{2,1,0:T(8,128)} %copy.115, f32[32,1,128]{2,1,0:T(1,128)S(1)} %collective-permute-done.19, f32[32,1,128]{2,1,0:T(1,128)S(1)} %collective-permute-done.18, ...), kind=kLoop, calls=%fused_computation.224 | loop fusion | flops 8650752 | bytes 4303904 | tf_op jit(solution)/shard_map/jit(_where)/select_n | solution.py:129
  125.0 3.5 collective-permute-start.24
  129.9 4.2 %collective-permute-done.25 = f32[32,1,128]{2,1,0:T(1,128)S(1)} collective-permute-done((f32[32,1,128]{2,1,0:T(1,128)S(1)}, f32[32,1,128]{2,1,0:T(1,128)S(1)}, u32[]{:S(2)}, u32[]{:S(2)}) %collective-permute-start.25) | collective-permute-done | bytes 16416 | tf_op jit(solution)/shard_map/ppermute | solution.py:21
  152.0 5.5 %fusion.83 = f32[32,32,128]{2,1,0:T(8,128)S(1)} fusion(f32[32,32,128]{2,1,0:T(8,128)} %copy-done.5, f32[32,32,128]{2,1,0:T(8,128)S(1)} %copy-done, f32[32,32,128]{2,1,0:T(8,128)S(1)} %get-tuple-element.9, f32[32,34,1]{2,1,0:T(8,128)} %copy.121, f32[32,1,128]{2,1,0:T(1,128)S(1)} %collective-permute-done.25, f32[32,1,128]{2,1,0:T(1,128)S(1)} %collective-permute-done.24, ...), kind=kLoop, calls=%fused_computation.192 | loop fusion | flops 8650752 | bytes 4303904 | tf_op jit(solution)/shard_map/jit(_where)/select_n | solution.py:129
  160.9 4.2 %collective-permute-done.31 = f32[32,1,128]{2,1,0:T(1,128)S(1)} collective-permute-done((f32[32,1,128]{2,1,0:T(1,128)S(1)}, f32[32,1,128]{2,1,0:T(1,128)S(1)}, u32[]{:S(2)}, u32[]{:S(2)}) %collective-permute-start.31) | collective-permute-done | bytes 16416 | tf_op jit(solution)/shard_map/ppermute | solution.py:21
  183.0 6.0 %fusion.69 = f32[32,32,128]{2,1,0:T(8,128)} fusion(f32[32,32,128]{2,1,0:T(8,128)S(1)} %copy-done, f32[32,32,128]{2,1,0:T(8,128)S(1)} %get-tuple-element.9, f32[32,34,1]{2,1,0:T(8,128)} %copy.127, f32[32,1,128]{2,1,0:T(1,128)S(1)} %collective-permute-done.31, f32[32,32,128]{2,1,0:T(8,128)} %copy-done.1, f32[32,1,128]{2,1,0:T(1,128)S(1)} %collective-permute-done.30, ...), kind=kLoop, calls=%fused_computation.160 | loop fusion | flops 6815744 | bytes 4303904 | tf_op jit(solution)/shard_map/sub | solution.py:136
  189.0 3.7 %reshape.108 = f32[2,16,2,16,8,16]{5,4,3,2,1,0:T(8,128)} reshape(f32[32,32,128]{2,1,0:T(8,128)} %fusion.69) | data formatting | bytes 1048576 | tf_op jit(solution)/shard_map/reshape | solution.py:138
  195.4 5.1 %all-gather = f32[8,2,8]{2,1,0:T(2,128)S(1)} all-gather(f32[2,2,8]{2,1,0:T(2,128)S(1)} %copy.130), channel_id=2, replica_groups=mesh['groups'=2,'gx'=4,'gy'=2,'gz'=2] {'gy','gz'}, dimensions={0}, use_global_device_ids=true | all-gather | bytes 640 | tf_op jit(solution)/shard_map/all_gather | solution.py:91
  205.7 4.8 %all-to-all-done = f32[2,4,16]{2,0,1:T(2,128)S(1)} async-done(((f32[2,4,16]{2,0,1:T(2,128)}), f32[2,4,16]{2,0,1:T(2,128)S(1)}, u32[]{:S(2)}, u32[]{:S(2)}) %all-to-all-start) | async-done | bytes 544 | tf_op jit(solution)/shard_map/all_to_all | solution.py:97
  211.6 3.2 all-to-all-start.1
  215.5 4.8 %all-to-all-done.1 = f32[4,2,16]{2,1,0:T(2,128)S(1)} async-done(((f32[4,2,16]{2,1,0:T(2,128)}), f32[4,2,16]{2,1,0:T(2,128)S(1)}, u32[]{:S(2)}, u32[]{:S(2)}) %all-to-all-start.1) | async-done | bytes 544 | tf_op jit(solution)/shard_map/all_to_all | solution.py:104
  223.5 3.9 %reshape.111 = f32[32,32,128]{2,1,0:T(8,128)} reshape(f32[2,16,2,16,8,16]{5,4,3,2,1,0:T(8,128)} %broadcast_in_dim.73) | data formatting | bytes 1048576 | tf_op jit(solution)/shard_map/reshape | solution.py:142
  232.6 4.2 %collective-permute-done.37 = f32[32,1,128]{2,1,0:T(1,128)S(1)} collective-permute-done((f32[32,1,128]{2,1,0:T(1,128)S(1)}, f32[32,1,128]{2,1,0:T(1,128)S(1)}, u32[]{:S(2)}, u32[]{:S(2)}) %collective-permute-start.37) | collective-permute-done | bytes 16416 | tf_op jit(solution)/shard_map/ppermute | solution.py:21
  255.2 5.5 %fusion.56 = f32[32,32,128]{2,1,0:T(8,128)S(1)} fusion(f32[32,32,128]{2,1,0:T(8,128)} %copy-done.3, f32[32,32,128]{2,1,0:T(8,128)S(1)} %copy-done, f32[32,32,128]{2,1,0:T(8,128)S(1)} %get-tuple-element.9, f32[32,34,1]{2,1,0:T(8,128)} %copy.139, f32[32,1,128]{2,1,0:T(1,128)S(1)} %collective-permute-done.37, f32[32,1,128]{2,1,0:T(1,128)S(1)} %collective-permute-done.36, ...), kind=kLoop, calls=%fused_computation.129 | loop fusion | flops 8650752 | bytes 4303904 | tf_op jit(solution)/shard_map/jit(_where)/select_n | solution.py:129
  264.6 4.2 %collective-permute-done.43 = f32[32,1,128]{2,1,0:T(1,128)S(1)} collective-permute-done((f32[32,1,128]{2,1,0:T(1,128)S(1)}, f32[32,1,128]{2,1,0:T(1,128)S(1)}, u32[]{:S(2)}, u32[]{:S(2)}) %collective-permute-start.43) | collective-permute-done | bytes 16416 | tf_op jit(solution)/shard_map/ppermute | solution.py:21
  286.7 5.5 %fusion.42 = f32[32,32,128]{2,1,0:T(8,128)S(1)} fusion(f32[32,32,128]{2,1,0:T(8,128)} %copy-done.7, f32[32,32,128]{2,1,0:T(8,128)S(1)} %copy-done, f32[32,32,128]{2,1,0:T(8,128)S(1)} %get-tuple-element.9, f32[32,34,1]{2,1,0:T(8,128)} %copy.145, f32[32,1,128]{2,1,0:T(1,128)S(1)} %collective-permute-done.43, f32[32,1,128]{2,1,0:T(1,128)S(1)} %collective-permute-done.42, ...), kind=kLoop, calls=%fused_computation.97 | loop fusion | flops 8650752 | bytes 4303904 | tf_op jit(solution)/shard_map/jit(_where)/select_n | solution.py:129
  296.1 4.2 %collective-permute-done.49 = f32[32,1,128]{2,1,0:T(1,128)S(1)} collective-permute-done((f32[32,1,128]{2,1,0:T(1,128)S(1)}, f32[32,1,128]{2,1,0:T(1,128)S(1)}, u32[]{:S(2)}, u32[]{:S(2)}) %collective-permute-start.49) | collective-permute-done | bytes 16416 | tf_op jit(solution)/shard_map/ppermute | solution.py:21
  318.3 5.5 %fusion.28 = f32[32,32,128]{2,1,0:T(8,128)S(1)} fusion(f32[32,32,128]{2,1,0:T(8,128)} %copy-done.8, f32[32,32,128]{2,1,0:T(8,128)S(1)} %copy-done, f32[32,32,128]{2,1,0:T(8,128)S(1)} %get-tuple-element.9, f32[32,34,1]{2,1,0:T(8,128)} %copy.151, f32[32,1,128]{2,1,0:T(1,128)S(1)} %collective-permute-done.49, f32[32,1,128]{2,1,0:T(1,128)S(1)} %collective-permute-done.48, ...), kind=kLoop, calls=%fused_computation.65 | loop fusion | flops 8650752 | bytes 4303904 | tf_op jit(solution)/shard_map/jit(_where)/select_n | solution.py:129
  327.1 4.2 %collective-permute-done.55 = f32[32,1,128]{2,1,0:T(1,128)S(1)} collective-permute-done((f32[32,1,128]{2,1,0:T(1,128)S(1)}, f32[32,1,128]{2,1,0:T(1,128)S(1)}, u32[]{:S(2)}, u32[]{:S(2)}) %collective-permute-start.55) | collective-permute-done | bytes 16416 | tf_op jit(solution)/shard_map/ppermute | solution.py:21
  349.3 6.4 %fusion.14 = f32[32,32,128]{2,1,0:T(8,128)} fusion(f32[32,32,128]{2,1,0:T(8,128)} %copy-done.4, f32[32,32,128]{2,1,0:T(8,128)S(1)} %copy-done, f32[32,32,128]{2,1,0:T(8,128)S(1)} %get-tuple-element.9, f32[32,34,1]{2,1,0:T(8,128)} %copy.157, f32[32,1,128]{2,1,0:T(1,128)S(1)} %collective-permute-done.55, f32[32,1,128]{2,1,0:T(1,128)S(1)} %collective-permute-done.54, ...), kind=kLoop, calls=%fused_computation.33 | loop fusion | flops 8650752 | bytes 4303904 | tf_op jit(solution)/shard_map/jit(_where)/select_n | solution.py:129
  (237 shorter events, 202.0 us)
Async XLA Ops:
  8.2 12.1 %collective-permute-start = (f32[32,1,128]{2,1,0:T(1,128)S(1)}, f32[32,1,128]{2,1,0:T(1,128)S(1)}, u32[]{:S(2)}, u32[]{:S(2)}) collective-permute-start(f32[32,1,128]{2,1,0:T(1,128)S(1)} %get-tuple-element.67), channel_id=1, source_target_pairs={{0,4},{4,8},{8,12},{1,5},{5,9},{9,13},{2,6},{6,10},{10,14},{3,7},{... | collective-permute-start | bytes 49160 | tf_op jit(solution)/shard_map/ppermute | solution.py:18
  13.2 7.2 %collective-permute-start.1 = (f32[32,1,128]{2,1,0:T(1,128)S(1)}, f32[32,1,128]{2,1,0:T(1,128)S(1)}, u32[]{:S(2)}, u32[]{:S(2)}) collective-permute-start(f32[32,1,128]{2,1,0:T(1,128)S(1)} %get-tuple-element.66), channel_id=1, source_target_pairs={{4,0},{8,4},{12,8},{5,1},{9,5},{13,9},{6,2},{10,6},{14,10},{7,3},{... | collective-permute-start | bytes 49160 | tf_op jit(solution)/shard_map/ppermute | solution.py:21
  14.5 11.5 %collective-permute-start.5 = (f32[32,1,128]{2,1,0:T(1,128)S(1)}, f32[32,1,128]{2,1,0:T(1,128)S(1)}, u32[]{:S(2)}, u32[]{:S(2)}) collective-permute-start(f32[32,1,128]{2,1,0:T(1,128)S(1)} %broadcast.221), channel_id=1, source_target_pairs={{0,4},{4,8},{8,12},{1,5},{5,9},{9,13},{2,6},{6,10},{10,14},{3,7},{... | collective-permute-start | bytes 49160 | tf_op jit(solution)/shard_map/ppermute | solution.py:18
  19.0 7.0 %collective-permute-start.6 = (f32[32,1,128]{2,1,0:T(1,128)S(1)}, f32[32,1,128]{2,1,0:T(1,128)S(1)}, u32[]{:S(2)}, u32[]{:S(2)}) collective-permute-start(f32[32,1,128]{2,1,0:T(1,128)S(1)} %broadcast.221), channel_id=1, source_target_pairs={{4,0},{8,4},{12,8},{5,1},{9,5},{13,9},{6,2},{10,6},{14,10},{7,3},{... | collective-permute-start | bytes 49160 | tf_op jit(solution)/shard_map/ppermute | solution.py:21
  21.0 13.9 %collective-permute-start.2 = (f32[32,34,1]{1,0,2:T(8,128)S(1)}, f32[32,34,1]{1,0,2:T(8,128)S(1)}, u32[]{:S(2)}, u32[]{:S(2)}) collective-permute-start(f32[32,34,1]{1,0,2:T(8,128)S(1)} %copy.94), channel_id=1, source_target_pairs={{0,2},{1,3},{4,6},{5,7},{8,10},{9,11},{12,14},{13,15},{16,18},{17,... | collective-permute-start | bytes 13064 | tf_op jit(solution)/shard_map/ppermute | solution.py:18
  24.7 10.5 %collective-permute-start.3 = (f32[32,34,1]{1,0,2:T(8,128)S(1)}, f32[32,34,1]{1,0,2:T(8,128)S(1)}, u32[]{:S(2)}, u32[]{:S(2)}) collective-permute-start(f32[32,34,1]{1,0,2:T(8,128)S(1)} %copy.95), channel_id=1, source_target_pairs={{2,0},{3,1},{6,4},{7,5},{10,8},{11,9},{14,12},{15,13},{18,16},{19,... | collective-permute-start | bytes 13064 | tf_op jit(solution)/shard_map/ppermute | solution.py:21
  28.7 11.3 %collective-permute-start.7 = (f32[32,34,1]{1,0,2:T(8,128)S(1)}, f32[32,34,1]{1,0,2:T(8,128)S(1)}, u32[]{:S(2)}, u32[]{:S(2)}) collective-permute-start(f32[32,34,1]{1,0,2:T(8,128)S(1)} %copy.98), channel_id=1, source_target_pairs={{0,2},{1,3},{4,6},{5,7},{8,10},{9,11},{12,14},{13,15},{16,18},{17,... | collective-permute-start | bytes 13064 | tf_op jit(solution)/shard_map/ppermute | solution.py:18
  33.6 7.7 %collective-permute-start.8 = (f32[32,34,1]{1,0,2:T(8,128)S(1)}, f32[32,34,1]{1,0,2:T(8,128)S(1)}, u32[]{:S(2)}, u32[]{:S(2)}) collective-permute-start(f32[32,34,1]{1,0,2:T(8,128)S(1)} %copy.99), channel_id=1, source_target_pairs={{2,0},{3,1},{6,4},{7,5},{10,8},{11,9},{14,12},{15,13},{18,16},{19,... | collective-permute-start | bytes 13064 | tf_op jit(solution)/shard_map/ppermute | solution.py:21
  35.7 11.9 %collective-permute-start.10 = (f32[1,34,130]{2,1,0:T(8,128)S(1)}, f32[1,34,130]{2,1,0:T(8,128)S(1)}, u32[]{:S(2)}, u32[]{:S(2)}) collective-permute-start(f32[1,34,130]{2,1,0:T(8,128)S(1)} %get-tuple-element.26), channel_id=1, source_target_pairs={{1,0},{3,2},{5,4},{7,6},{9,8},{11,10},{13,12},{15,14},{17,16},{19,... | collective-permute-start | bytes 53048 | tf_op jit(solution)/shard_map/ppermute | solution.py:21
  37.0 10.7 %collective-permute-start.4 = (f32[1,34,130]{2,1,0:T(8,128)S(1)}, f32[1,34,130]{2,1,0:T(8,128)S(1)}, u32[]{:S(2)}, u32[]{:S(2)}) collective-permute-start(f32[1,34,130]{2,1,0:T(8,128)S(1)} %get-tuple-element.27), channel_id=1, source_target_pairs={{0,1},{2,3},{4,5},{6,7},{8,9},{10,11},{12,13},{14,15},{16,17},{18,... | collective-permute-start | bytes 53048 | tf_op jit(solution)/shard_map/ppermute | solution.py:18
  55.9 6.0 %collective-permute-start.12 = (f32[32,1,128]{2,1,0:T(1,128)S(1)}, f32[32,1,128]{2,1,0:T(1,128)S(1)}, u32[]{:S(2)}, u32[]{:S(2)}) collective-permute-start(f32[32,1,128]{2,1,0:T(1,128)S(1)} %get-tuple-element.64), channel_id=1, source_target_pairs={{0,4},{4,8},{8,12},{1,5},{5,9},{9,13},{2,6},{6,10},{10,14},{3,7},{... | collective-permute-start | bytes 49160 | tf_op jit(solution)/shard_map/ppermute | solution.py:18
  60.4 5.6 %collective-permute-start.13 = (f32[32,1,128]{2,1,0:T(1,128)S(1)}, f32[32,1,128]{2,1,0:T(1,128)S(1)}, u32[]{:S(2)}, u32[]{:S(2)}) collective-permute-start(f32[32,1,128]{2,1,0:T(1,128)S(1)} %get-tuple-element.65), channel_id=1, source_target_pairs={{4,0},{8,4},{12,8},{5,1},{9,5},{13,9},{6,2},{10,6},{14,10},{7,3},{... | collective-permute-start | bytes 49160 | tf_op jit(solution)/shard_map/ppermute | solution.py:21
  68.8 7.2 %collective-permute-start.14 = (f32[32,34,1]{1,0,2:T(8,128)S(1)}, f32[32,34,1]{1,0,2:T(8,128)S(1)}, u32[]{:S(2)}, u32[]{:S(2)}) collective-permute-start(f32[32,34,1]{1,0,2:T(8,128)S(1)} %copy.106), channel_id=1, source_target_pairs={{0,2},{1,3},{4,6},{5,7},{8,10},{9,11},{12,14},{13,15},{16,18},{17,... | collective-permute-start | bytes 13064 | tf_op jit(solution)/shard_map/ppermute | solution.py:18
  74.8 5.6 %collective-permute-start.15 = (f32[32,34,1]{1,0,2:T(8,128)S(1)}, f32[32,34,1]{1,0,2:T(8,128)S(1)}, u32[]{:S(2)}, u32[]{:S(2)}) collective-permute-start(f32[32,34,1]{1,0,2:T(8,128)S(1)} %copy.107), channel_id=1, source_target_pairs={{2,0},{3,1},{6,4},{7,5},{10,8},{11,9},{14,12},{15,13},{18,16},{19,... | collective-permute-start | bytes 13064 | tf_op jit(solution)/shard_map/ppermute | solution.py:21
  92.4 4.9 %collective-permute-start.18 = (f32[32,1,128]{2,1,0:T(1,128)S(1)}, f32[32,1,128]{2,1,0:T(1,128)S(1)}, u32[]{:S(2)}, u32[]{:S(2)}) collective-permute-start(f32[32,1,128]{2,1,0:T(1,128)S(1)} %get-tuple-element.62), channel_id=1, source_target_pairs={{0,4},{4,8},{8,12},{1,5},{5,9},{9,13},{2,6},{6,10},{10,14},{3,7},{... | collective-permute-start | bytes 49160 | tf_op jit(solution)/shard_map/ppermute | solution.py:18
  95.9 5.6 %collective-permute-start.19 = (f32[32,1,128]{2,1,0:T(1,128)S(1)}, f32[32,1,128]{2,1,0:T(1,128)S(1)}, u32[]{:S(2)}, u32[]{:S(2)}) collective-permute-start(f32[32,1,128]{2,1,0:T(1,128)S(1)} %get-tuple-element.63), channel_id=1, source_target_pairs={{4,0},{8,4},{12,8},{5,1},{9,5},{13,9},{6,2},{10,6},{14,10},{7,3},{... | collective-permute-start | bytes 49160 | tf_op jit(solution)/shard_map/ppermute | solution.py:21
  107.3 5.6 %collective-permute-start.21 = (f32[32,34,1]{1,0,2:T(8,128)S(1)}, f32[32,34,1]{1,0,2:T(8,128)S(1)}, u32[]{:S(2)}, u32[]{:S(2)}) collective-permute-start(f32[32,34,1]{1,0,2:T(8,128)S(1)} %copy.113), channel_id=1, source_target_pairs={{2,0},{3,1},{6,4},{7,5},{10,8},{11,9},{14,12},{15,13},{18,16},{19,... | collective-permute-start | bytes 13064 | tf_op jit(solution)/shard_map/ppermute | solution.py:21
  125.0 4.9 %collective-permute-start.24 = (f32[32,1,128]{2,1,0:T(1,128)S(1)}, f32[32,1,128]{2,1,0:T(1,128)S(1)}, u32[]{:S(2)}, u32[]{:S(2)}) collective-permute-start(f32[32,1,128]{2,1,0:T(1,128)S(1)} %get-tuple-element.60), channel_id=1, source_target_pairs={{0,4},{4,8},{8,12},{1,5},{5,9},{9,13},{2,6},{6,10},{10,14},{3,7},{... | collective-permute-start | bytes 49160 | tf_op jit(solution)/shard_map/ppermute | solution.py:18
  128.5 5.6 %collective-permute-start.25 = (f32[32,1,128]{2,1,0:T(1,128)S(1)}, f32[32,1,128]{2,1,0:T(1,128)S(1)}, u32[]{:S(2)}, u32[]{:S(2)}) collective-permute-start(f32[32,1,128]{2,1,0:T(1,128)S(1)} %get-tuple-element.61), channel_id=1, source_target_pairs={{4,0},{8,4},{12,8},{5,1},{9,5},{13,9},{6,2},{10,6},{14,10},{7,3},{... | collective-permute-start | bytes 49160 | tf_op jit(solution)/shard_map/ppermute | solution.py:21
  139.9 5.6 %collective-permute-start.27 = (f32[32,34,1]{1,0,2:T(8,128)S(1)}, f32[32,34,1]{1,0,2:T(8,128)S(1)}, u32[]{:S(2)}, u32[]{:S(2)}) collective-permute-start(f32[32,34,1]{1,0,2:T(8,128)S(1)} %copy.119), channel_id=1, source_target_pairs={{2,0},{3,1},{6,4},{7,5},{10,8},{11,9},{14,12},{15,13},{18,16},{19,... | collective-permute-start | bytes 13064 | tf_op jit(solution)/shard_map/ppermute | solution.py:21
  159.5 5.6 %collective-permute-start.31 = (f32[32,1,128]{2,1,0:T(1,128)S(1)}, f32[32,1,128]{2,1,0:T(1,128)S(1)}, u32[]{:S(2)}, u32[]{:S(2)}) collective-permute-start(f32[32,1,128]{2,1,0:T(1,128)S(1)} %get-tuple-element.59), channel_id=1, source_target_pairs={{4,0},{8,4},{12,8},{5,1},{9,5},{13,9},{6,2},{10,6},{14,10},{7,3},{... | collective-permute-start | bytes 49160 | tf_op jit(solution)/shard_map/ppermute | solution.py:21
  170.9 5.6 %collective-permute-start.33 = (f32[32,34,1]{1,0,2:T(8,128)S(1)}, f32[32,34,1]{1,0,2:T(8,128)S(1)}, u32[]{:S(2)}, u32[]{:S(2)}) collective-permute-start(f32[32,34,1]{1,0,2:T(8,128)S(1)} %copy.125), channel_id=1, source_target_pairs={{2,0},{3,1},{6,4},{7,5},{10,8},{11,9},{14,12},{15,13},{18,16},{19,... | collective-permute-start | bytes 13064 | tf_op jit(solution)/shard_map/ppermute | solution.py:21
  201.7 8.8 %all-to-all-start = ((f32[2,4,16]{2,0,1:T(2,128)}), f32[2,4,16]{2,0,1:T(2,128)S(1)}, u32[]{:S(2)}, u32[]{:S(2)}) async-start(f32[2,4,16]{2,0,1:T(2,128)} %fusion.142), calls=%async_computation | async-start | bytes 8192 | tf_op jit(solution)/shard_map/all_to_all | solution.py:97
  211.6 8.8 %all-to-all-start.1 = ((f32[4,2,16]{2,1,0:T(2,128)}), f32[4,2,16]{2,1,0:T(2,128)S(1)}, u32[]{:S(2)}, u32[]{:S(2)}) async-start(f32[4,2,16]{2,1,0:T(2,128)} %bitcast.16), calls=%async_computation.1 | async-start | bytes 8192 | tf_op jit(solution)/shard_map/all_to_all | solution.py:104
  231.2 5.6 %collective-permute-start.37 = (f32[32,1,128]{2,1,0:T(1,128)S(1)}, f32[32,1,128]{2,1,0:T(1,128)S(1)}, u32[]{:S(2)}, u32[]{:S(2)}) collective-permute-start(f32[32,1,128]{2,1,0:T(1,128)S(1)} %get-tuple-element.57), channel_id=1, source_target_pairs={{4,0},{8,4},{12,8},{5,1},{9,5},{13,9},{6,2},{10,6},{14,10},{7,3},{... | collective-permute-start | bytes 49160 | tf_op jit(solution)/shard_map/ppermute | solution.py:21
  243.0 5.6 %collective-permute-start.39 = (f32[32,34,1]{1,0,2:T(8,128)S(1)}, f32[32,34,1]{1,0,2:T(8,128)S(1)}, u32[]{:S(2)}, u32[]{:S(2)}) collective-permute-start(f32[32,34,1]{1,0,2:T(8,128)S(1)} %copy.137), channel_id=1, source_target_pairs={{2,0},{3,1},{6,4},{7,5},{10,8},{11,9},{14,12},{15,13},{18,16},{19,... | collective-permute-start | bytes 13064 | tf_op jit(solution)/shard_map/ppermute | solution.py:21
  263.2 5.6 %collective-permute-start.43 = (f32[32,1,128]{2,1,0:T(1,128)S(1)}, f32[32,1,128]{2,1,0:T(1,128)S(1)}, u32[]{:S(2)}, u32[]{:S(2)}) collective-permute-start(f32[32,1,128]{2,1,0:T(1,128)S(1)} %get-tuple-element.55), channel_id=1, source_target_pairs={{4,0},{8,4},{12,8},{5,1},{9,5},{13,9},{6,2},{10,6},{14,10},{7,3},{... | collective-permute-start | bytes 49160 | tf_op jit(solution)/shard_map/ppermute | solution.py:21
  274.6 5.6 %collective-permute-start.45 = (f32[32,34,1]{1,0,2:T(8,128)S(1)}, f32[32,34,1]{1,0,2:T(8,128)S(1)}, u32[]{:S(2)}, u32[]{:S(2)}) collective-permute-start(f32[32,34,1]{1,0,2:T(8,128)S(1)} %copy.143), channel_id=1, source_target_pairs={{2,0},{3,1},{6,4},{7,5},{10,8},{11,9},{14,12},{15,13},{18,16},{19,... | collective-permute-start | bytes 13064 | tf_op jit(solution)/shard_map/ppermute | solution.py:21
  294.7 5.6 %collective-permute-start.49 = (f32[32,1,128]{2,1,0:T(1,128)S(1)}, f32[32,1,128]{2,1,0:T(1,128)S(1)}, u32[]{:S(2)}, u32[]{:S(2)}) collective-permute-start(f32[32,1,128]{2,1,0:T(1,128)S(1)} %get-tuple-element.53), channel_id=1, source_target_pairs={{4,0},{8,4},{12,8},{5,1},{9,5},{13,9},{6,2},{10,6},{14,10},{7,3},{... | collective-permute-start | bytes 49160 | tf_op jit(solution)/shard_map/ppermute | solution.py:21
  306.1 5.6 %collective-permute-start.51 = (f32[32,34,1]{1,0,2:T(8,128)S(1)}, f32[32,34,1]{1,0,2:T(8,128)S(1)}, u32[]{:S(2)}, u32[]{:S(2)}) collective-permute-start(f32[32,34,1]{1,0,2:T(8,128)S(1)} %copy.149), channel_id=1, source_target_pairs={{2,0},{3,1},{6,4},{7,5},{10,8},{11,9},{14,12},{15,13},{18,16},{19,... | collective-permute-start | bytes 13064 | tf_op jit(solution)/shard_map/ppermute | solution.py:21
  325.7 5.6 %collective-permute-start.55 = (f32[32,1,128]{2,1,0:T(1,128)S(1)}, f32[32,1,128]{2,1,0:T(1,128)S(1)}, u32[]{:S(2)}, u32[]{:S(2)}) collective-permute-start(f32[32,1,128]{2,1,0:T(1,128)S(1)} %get-tuple-element.51), channel_id=1, source_target_pairs={{4,0},{8,4},{12,8},{5,1},{9,5},{13,9},{6,2},{10,6},{14,10},{7,3},{... | collective-permute-start | bytes 49160 | tf_op jit(solution)/shard_map/ppermute | solution.py:21
  337.1 5.6 %collective-permute-start.57 = (f32[32,34,1]{1,0,2:T(8,128)S(1)}, f32[32,34,1]{1,0,2:T(8,128)S(1)}, u32[]{:S(2)}, u32[]{:S(2)}) collective-permute-start(f32[32,34,1]{1,0,2:T(8,128)S(1)} %copy.155), channel_id=1, source_target_pairs={{2,0},{3,1},{6,4},{7,5},{10,8},{11,9},{14,12},{15,13},{18,16},{19,... | collective-permute-start | bytes 13064 | tf_op jit(solution)/shard_map/ppermute | solution.py:21
  (43 other events, 250.0 us)
where the time goes:
time: 359 us; the launch traced here: 356 us
  starting transfers between devices  118 us (33%)
  waiting for transfers between devices  84.3 us (23%)
  other arithmetic  72.9 us (20%)
  local copies, waits for them, and re-layouts  70.3 us (20%)
  blocking collectives  5.15 us (1%)
    ppermute x30, starting transfers between devices, padded_2(): lax.ppermute(lax.slice_in_dim(block, block.shape[dim] - width, None, axis...  72.9 us
    ppermute x30, waiting for transfers between devices, padded_2(): lax.ppermute(lax.slice_in_dim(block, 0, width, axis=dim), axis, backward)  72.9 us
    select_n x8, other arithmetic, sweep(): jnp.where(mask, (heat + neighbour_sum(weights, upad, shape, 1)) / diag, f...  46.5 us
    ppermute x30, starting transfers between devices, padded_2(): lax.ppermute(lax.slice_in_dim(block, 0, width, axis=dim), axis, backward)  39.1 us
    slice x28, local copies, waits for them, and re-layouts, padded_2(): lax.slice_in_dim(block, block.shape[dim] - width, None, axis=dim)  24.5 us
    slice x11, local copies, waits for them, and re-layouts, padded_2(): lax.slice_in_dim(block, 0, width, axis=dim)  11.9 us
    ppermute x10, local copies, waits for them, and re-layouts, padded_2(): lax.ppermute(lax.slice_in_dim(block, 0, width, axis=dim), axis, backward)  11.1 us
    ppermute x10, local copies, waits for them, and re-layouts, padded_2(): lax.ppermute(lax.slice_in_dim(block, block.shape[dim] - width, None, axis...  10.9 us
  transfers between devices with their start and end apart: 62, of which 35 were waited for; matrix products, arithmetic and copies ran while one was open for 8% of the time, Pallas kernels for 0%

commit v1 on v0

v1 whole, which is shorter than its diff:
```python
import functools
import math

import jax
import jax.numpy as jnp
import numpy as np
from jax import lax
from jax.experimental import pallas as pl
from jax.experimental.pallas import tpu as pltpu
from jax.sharding import PartitionSpec as P

BLOCK = 16
PAD = 8
MESH = pl.DeviceIdType.MESH
HIGH = lax.Precision.HIGHEST
ROUNDS = 8


def sine_rows(count):
    j = np.arange(-1, count + 1)[:, None] + 1.0
    k = np.arange(count)[None, :] + 1.0
    rows = np.sin(math.pi * j * k / (count + 1))
    rows[0] = 0.0
    rows[-1] = 0.0
    return rows


def tables(shape, n_gx, n_gy, n_gz):
    lz, lx, ly = (s // BLOCK for s in shape)
    fz, fx, fy = lz * n_gz, lx * n_gx, ly * n_gy
    cols = fz * fy
    wide = -(-cols // 128) * 128
    sz, sx, sy = sine_rows(fz), sine_rows(fx), sine_rows(fy)
    zs = np.arange(-1, shape[0] + 1)
    ys = np.arange(-1, shape[2] + 1)
    spread = np.zeros((n_gy, n_gz, wide, (lz + 4) * 128))
    gather = np.zeros((n_gy, n_gz, lz * 128, wide))
    for a in range(n_gy):
        yrow = np.floor_divide(ys + a * shape[2], BLOCK) + 1
        for b in range(n_gz):
            zrow = np.arange(-1, lz + 1) + b * lz + 1
            for i, row in enumerate(zrow):
                block = np.einsum("p,yq->pqy", sz[row], sy[yrow[1:-1]]).reshape(cols, -1)
                spread[a, b, :cols, i * 128 : i * 128 + shape[2]] = block
                if 1 <= i <= lz:
                    gather[a, b, (i - 1) * 128 : i * 128, :cols] = block.T
            fine = np.floor_divide(np.arange(shape[0]) + b * shape[0], BLOCK) + 1
            for side, row in ((0, yrow[0]), (1, yrow[-1])):
                block = np.einsum("zp,q->pqz", sz[fine], sy[row]).reshape(cols, -1)
                at = (lz + 2 + side) * 128
                spread[a, b, :cols, at : at + shape[0]] = block
    rows = shape[1] + 2 * PAD
    expand = np.zeros((n_gx, rows, fx))
    shrink = np.zeros((n_gx, fx, shape[1]))
    for a in range(n_gx):
        xs = np.arange(-1, shape[1] + 1) + a * shape[1]
        block = sx[np.floor_divide(xs, BLOCK) + 1]
        expand[a, PAD - 1 : PAD + shape[1] + 1] = block
        shrink[a] = block[1:-1].T
    lam = lambda n: 2.0 - 2.0 * np.cos(math.pi * (np.arange(n) + 1.0) / (n + 1))
    total = lam(fx)[:, None] + (lam(fz)[:, None] + lam(fy)[None, :]).reshape(1, -1)
    scale = np.zeros((fx, wide))
    scale[:, :cols] = BLOCK * BLOCK * 8.0 / ((fz + 1) * (fx + 1) * (fy + 1)) / total / BLOCK**3
    return [t.astype(np.float32) for t in (spread, gather, expand, shrink, scale)]


def kernel(
    sizes, shape, heat, mat, table, spread_hbm, gather_hbm, expand_hbm, shrink_hbm, scale,
    out, kp, u, wd, hd, dg, vsum, corr, spread, gather, expand, shrink,
    s_z, r_z, s_x, r_x, s_y, r_y, got, tab_sem, send_sem, recv_sem, gsend, grecv,
):
    n_gx, n_gy, n_gz = sizes
    nz, nx, ny = shape
    lz = nz // BLOCK
    rows = nx + 2 * PAD
    gx, gy, gz = lax.axis_index("gx"), lax.axis_index("gy"), lax.axis_index("gz")
    count = n_gx * n_gy * n_gz
    me = (gx * n_gy + gy) * n_gz + gz

    def peer_of(step):
        other = lax.rem(me + step, count)
        return other, {
            "gx": other // (n_gy * n_gz),
            "gy": lax.rem(other // n_gz, n_gy),
            "gz": lax.rem(other, n_gz),
        }

    barrier = pltpu.get_barrier_semaphore()

    def greet(step, carry):
        _, where = peer_of(step)
        pl.semaphore_signal(barrier, inc=1, device_id=where, device_id_type=MESH)
        return carry

    lax.fori_loop(1, count, greet, 0)

    fetch = [
        pltpu.make_async_copy(spread_hbm.at[gy, gz], spread, tab_sem.at[0]),
        pltpu.make_async_copy(gather_hbm.at[gy, gz], gather, tab_sem.at[1]),
        pltpu.make_async_copy(expand_hbm.at[gx], expand, tab_sem.at[2]),
        pltpu.make_async_copy(shrink_hbm.at[gx], shrink, tab_sem.at[3]),
    ]
    for copy in fetch:
        copy.start()

    faces = []
    for bufs, name, index, size, sem in (
        ((s_z, r_z), "gz", gz, n_gz, 0),
        ((s_x, r_x), "gx", gx, n_gx, 2),
    ):
        if size > 1:
            faces.append((*bufs, 0, 1, index > 0, {name: index - 1}, sem))
            faces.append((*bufs, 1, 0, index < size - 1, {name: index + 1}, sem + 1))
    single = n_gy == 2
    if single:
        edge = (ny - 1) * (1 - gy)
        edges = [edge]
        faces.append((s_y, r_y, 0, 0, None, {"gy": 1 - gy}, 4))
    else:
        edges = [0, ny - 1]
        if n_gy > 1:
            faces.append((s_y, r_y, 0, 1, gy > 0, {"gy": gy - 1}, 4))
            faces.append((s_y, r_y, 1, 0, gy < n_gy - 1, {"gy": gy + 1}, 5))

    def copies(turn, landing):
        for src, dst, mine, theirs, exists, where, sem in faces:
            there = sem if single and sem == 4 else (sem // 2) * 2 + theirs
            yield exists, pltpu.make_async_remote_copy(
                src_ref=src.at[turn, mine],
                dst_ref=dst.at[turn, mine if landing else theirs],
                send_sem=send_sem.at[turn, sem],
                recv_sem=recv_sem.at[turn, sem if landing else there],
                device_id=where,
                device_id_type=MESH,
            )

    def guarded(exists, action):
        if exists is None:
            action()
        else:
            pl.when(exists)(action)

    lane = lax.broadcasted_iota(jnp.int32, (nx, ny), 1)
    row = lax.broadcasted_iota(jnp.int32, (nx, ny), 0)
    odd = lax.rem(lane + row, 2)
    zero = jnp.zeros((nx, ny), jnp.float32)
    for buf, size, index in ((r_z, n_gz, gz), (r_x, n_gx, gx), (r_y, n_gy, gy)):
        if buf is r_y and single:
            continue
        for side, at in ((0, 0), (1, size - 1)):
            def clear(buf=buf, side=side):
                for turn in range(ROUNDS):
                    buf[turn, side] = jnp.zeros(buf.shape[2:], jnp.float32)

            pl.when(index == at)(clear)

    def slab(z):
        return pl.ds(pl.multiple_of(z * rows, 8) + PAD, nx)

    def packed(packs, value, z):
        result = []
        for pack, at in zip(packs, edges):
            turned = pltpu.roll(value, lax.rem(z - at + ny, ny), 1)
            result.append(jnp.where(lane == z, turned, pack))
        return tuple(result)

    blank = tuple(zero for _ in edges)

    def send(turn, field, packs):
        s_z[turn, 0] = field[pl.ds(rows + PAD, nx), :]
        s_z[turn, 1] = field[pl.ds(nz * rows + PAD, nx), :]
        for side, at in ((0, PAD), (1, PAD + nx - 1)):
            s_x[turn, side] = field[pl.ds(rows + at, nz, stride=rows), :]
        for side, pack in enumerate(packs):
            s_y[turn, side] = pack
        for exists, copy in copies(turn, False):
            guarded(exists, copy.start)

    def receive(turn, field):
        for exists, copy in copies(turn, True):
            guarded(exists, copy.wait_recv)
        field[pl.ds(PAD, nx), :] = r_z[turn, 0]
        field[pl.ds((nz + 1) * rows + PAD, nx), :] = r_z[turn, 1]
        for side, at in ((0, PAD - 1), (1, PAD + nx)):
            field[pl.ds(rows + at, nz, stride=rows), :] = r_x[turn, side]

    def beside(value, halos, z, strict):
        low, high = pltpu.roll(value, 1, 1), pltpu.roll(value, ny - 1, 1)
        if single:
            halo = pltpu.roll(halos[0], lax.rem(edge - z + ny, ny), 1)
            if strict:
                outer = gy.astype(jnp.float32)
                return (
                    jnp.where(lane == 0, halo * outer, low),
                    jnp.where(lane == ny - 1, halo * (1.0 - outer), high),
                )
            return jnp.where(lane == 0, halo, low), jnp.where(lane == ny - 1, halo, high)
        if n_gy == 1:
            return jnp.where(lane == 0, 0.0, low), jnp.where(lane == ny - 1, 0.0, high)
        first = pltpu.roll(halos[0], lax.rem(ny - z, ny), 1)
        last = pltpu.roll(halos[1], lax.rem(2 * ny - 1 - z, ny), 1)
        return jnp.where(lane == 0, first, low), jnp.where(lane == ny - 1, last, high)

    def around(field, halos, z, strict=False):
        value = field[slab(z + 1), :]
        low, high = beside(value, halos, z, strict)
        at = pl.multiple_of((z + 1) * rows, 8) + PAD
        return value, (
            field[slab(z), :],
            field[slab(z + 2), :],
            field[pl.ds(at - 1, nx), :],
            field[pl.ds(at + 1, nx), :],
            low,
            high,
        )

    def y_halos(turn):
        return [r_y[turn, side] for side in range(len(edges))]

    def conduct(z, packs):
        ids = mat[z]
        value = jnp.full((nx, ny), table[0], jnp.float32)
        for m in range(1, table.shape[0]):
            value = jnp.where(ids == m, table[m], value)
        kp[slab(z + 1), :] = value
        return packed(packs, value, z)

    packs = lax.fori_loop(0, nz, conduct, blank, unroll=2)
    pl.semaphore_wait(barrier, count - 1)
    send(0, kp, packs)
    receive(0, kp)
    halos = y_halos(0)

    def weigh(z, packs):
        center, others = around(kp, halos, z, True)
        diag = None
        inner = []
        for other in others:
            inside = other > 0.0
            weight = 2.0 * center * other / (center + other)
            full = jnp.where(inside, weight, center)
            inner.append(jnp.where(inside, weight, 0.0))
            diag = full if diag is None else diag + full
        inverse = 1.0 / diag
        for face in range(6):
            wd[face, z] = inner[face] * inverse
        ratio = heat[z] * inverse
        hd[z] = ratio
        dg[z] = diag
        value = jnp.where(odd == lax.rem(z, 2), ratio, 0.0)
        u[slab(z + 1), :] = value
        return packed(packs, value, z)

    packs = lax.fori_loop(0, nz, weigh, blank)
    send(1, u, packs)

    def total(z, halos):
        value, others = around(u, halos, z)
        result = hd[z]
        for face in range(6):
            result = result + wd[face, z] * others[face]
        return value, result

    def half(color, halos, last=False):
        def step(z, packs):
            value, result = total(z, halos)
            value = jnp.where(odd == lax.rem(z + color, 2), result, value)
            if last:
                out[z] = value
                return packs
            u[slab(z + 1), :] = value
            return packed(packs, value, z)

        return lax.fori_loop(0, nz, step, blank, unroll=2)

    for turn, color in ((2, 1), (3, 0), (4, 1)):
        receive(turn - 1, u)
        packs = half(color, y_halos(turn - 1))
        send(turn, u, packs)
    receive(4, u)
    halos = y_halos(4)

    for layer in range(lz):
        def gap(z, acc):
            value, result = total(z, halos)
            return acc + jnp.where(odd == lax.rem(z, 2), dg[z] * (result - value), 0.0)

        vsum[:, layer * ny : (layer + 1) * ny] = lax.fori_loop(
            layer * BLOCK, (layer + 1) * BLOCK, gap, zero, unroll=2
        )
    for copy in fetch:
        copy.wait()
    part = jnp.dot(shrink[...], vsum[...], precision=HIGH, preferred_element_type=jnp.float32)
    part = jnp.dot(part, gather[...], precision=HIGH, preferred_element_type=jnp.float32)
    got[me] = part

    def gathering(step, start):
        other, where = peer_of(step)
        copy = pltpu.make_async_remote_copy(
            src_ref=got.at[me],
            dst_ref=got.at[me if start else other],
            send_sem=gsend.at[step],
            recv_sem=grecv.at[me if start else other],
            device_id=where,
            device_id_type=MESH,
        )
        return copy

    def give(step, carry):
        gathering(step, True).start()
        return carry

    def take(step, carry):
        gathering(step, False).wait_recv()
        return carry

    lax.fori_loop(1, count, give, 0)
    lax.fori_loop(1, count, take, 0)
    if count <= 32:
        hat = got[0]
        for i in range(1, count):
            hat = hat + got[i]
    else:
        hat = lax.fori_loop(1, count, lambda i, acc: acc + got[i], got[0])
    kbar = table[0]
    for m in range(1, table.shape[0]):
        kbar = kbar + table[m]
    kbar = kbar / table.shape[0]
    hat = hat * scale[...] / kbar
    hat = jnp.dot(hat, spread[...], precision=HIGH, preferred_element_type=jnp.float32)
    corr[...] = jnp.dot(expand[...], hat, precision=HIGH, preferred_element_type=jnp.float32)

    def correct(z, carry):
        layer = (z + BLOCK - 1) // BLOCK
        at = pl.ds(pl.multiple_of(z * rows, 8), rows)
        u[at, :] = u[at, :] + corr[:, pl.ds(pl.multiple_of(layer * ny, ny), ny)]
        return carry

    lax.fori_loop(0, nz + 2, correct, 0, unroll=2)
    sides = [corr[PAD : PAD + nx, (lz + 2 + s) * ny : (lz + 3 + s) * ny] for s in range(2)]
    if single:
        upper = gy.astype(jnp.float32)
        halos = [halos[0] + sides[0] * upper + sides[1] * (1.0 - upper)]
    else:
        halos = [halo + side for halo, side in zip(halos, sides)]

    packs = half(0, halos)
    send(5, u, packs)
    for turn, color in ((6, 1), (7, 0)):
        receive(turn - 1, u)
        packs = half(color, y_halos(turn - 1))
        send(turn, u, packs)
    receive(7, u)
    half(1, y_halos(7), True)

    for turn in range(ROUNDS):
        for exists, copy in copies(turn, False):
            guarded(exists, copy.wait_send)

    def sent(step, carry):
        gathering(step, True).wait_send()
        return carry

    lax.fori_loop(1, count, sent, 0)


def per_device(sizes, heat, material, table):
    shape = heat.shape
    nz, nx, ny = shape
    n_gx, n_gy, n_gz = sizes
    consts = tables(shape, *sizes)
    spread, gather, expand, shrink, scale = consts
    count = n_gx * n_gy * n_gz
    rows = nx + 2 * PAD
    sides = 1 if n_gy == 2 else 2
    f32 = jnp.float32
    vmem = pl.BlockSpec(memory_space=pltpu.VMEM)
    hbm = pl.BlockSpec(memory_space=pl.ANY)
    faces = [
        pltpu.VMEM((ROUNDS, 2, nx, ny), f32),
        pltpu.VMEM((ROUNDS, 2, nx, ny), f32),
        pltpu.VMEM((ROUNDS, 2, nz, ny), f32),
        pltpu.VMEM((ROUNDS, 2, nz, ny), f32),
        pltpu.VMEM((ROUNDS, sides, nx, ny), f32),
        pltpu.VMEM((ROUNDS, sides, nx, ny), f32),
    ]
    return pl.pallas_call(
        functools.partial(kernel, sizes, shape),
        out_shape=jax.ShapeDtypeStruct(shape, f32),
        in_specs=[vmem, vmem, pl.BlockSpec(memory_space=pltpu.SMEM), hbm, hbm, hbm, hbm, vmem],
        out_specs=vmem,
        scratch_shapes=[
            pltpu.VMEM(((nz + 2) * rows, ny), f32),
            pltpu.VMEM(((nz + 2) * rows, ny), f32),
            pltpu.VMEM((6, nz, nx, ny), f32),
            pltpu.VMEM(shape, f32),
            pltpu.VMEM(shape, f32),
            pltpu.VMEM((nx, nz // BLOCK * ny), f32),
            pltpu.VMEM((rows, spread.shape[3]), f32),
            pltpu.VMEM(spread.shape[2:], f32),
            pltpu.VMEM(gather.shape[2:], f32),
            pltpu.VMEM(expand.shape[1:], f32),
            pltpu.VMEM(shrink.shape[1:], f32),
            *faces,
            pltpu.VMEM((count, *scale.shape), f32),
            pltpu.SemaphoreType.DMA((4,)),
            pltpu.SemaphoreType.DMA((ROUNDS, 6)),
            pltpu.SemaphoreType.DMA((ROUNDS, 6)),
            pltpu.SemaphoreType.DMA((count,)),
            pltpu.SemaphoreType.DMA((count,)),
        ],
        compiler_params=pltpu.CompilerParams(
            collective_id=0, has_side_effects=True, vmem_limit_bytes=50 * 1024 * 1024
        ),
    )(heat, material, table, *(jnp.asarray(c) for c in consts))


def solution(mesh):
    sizes = (mesh.shape["gx"], mesh.shape["gy"], mesh.shape["gz"])
    spec = P("gz", ("groups", "gx"), "gy")
    return jax.shard_map(
        functools.partial(per_device, sizes),
        mesh=mesh,
        in_specs=(spec, spec, P()),
        out_specs=spec,
        check_vma=False,
    )
```

time: 359 us -> 68.2 us (0.19)
  starting transfers between devices: 118 us -> 0 us
  waiting for transfers between devices: 84.3 us -> 0 us
  other arithmetic: 72.9 us -> 0 us
  local copies, waits for them, and re-layouts: 70.3 us -> 8.28 us
  Pallas kernels: 0 us -> 59.5 us
  blocking collectives: 5.15 us -> 0 us
    ppermute x60 -> x0, starting transfers between devices: 112 us -> none  [the longest x30 72.9 us: padded_2(): lax.ppermute(lax.slice_in_dim(block, block.shape[dim] - width, None, axis...]
    ppermute x60 -> x0, waiting for transfers between devices: 74.7 us -> none  [the longest x30 72.9 us: padded_2(): lax.ppermute(lax.slice_in_dim(block, 0, width, axis=dim), axis, backward)]
    pallas_call x0 -> x1, Pallas kernels: none -> 59.5 us  [per_device(): pl.pallas_call(functools.partial(kernel, sizes, shape), out_shape=jax.Sha...]
    select_n x8 -> x0, other arithmetic: 46.5 us -> none  [sweep(): jnp.where(mask, (heat + neighbour_sum(weights, upad, shape, 1)) / diag, f...]
    slice x40 -> x0, local copies, waits for them, and re-layouts: 38 us -> none  [the longest x28 24.5 us: padded_2(): lax.slice_in_dim(block, block.shape[dim] - width, None, axis=dim)]
    ppermute x20 -> x0, local copies, waits for them, and re-layouts: 22 us -> none  [the longest x10 11.1 us: padded_2(): lax.ppermute(lax.slice_in_dim(block, 0, width, axis=dim), axis, backward)]
    all_to_all x2 -> x0, waiting for transfers between devices: 9.61 us -> none  [the longest x1 4.82 us: coarse_block(): back = lax.all_to_all(turned, 'gx', split_axis=0, concat_axis=1, tiled=True)]
    unnamed x26 -> x17, local copies, waits for them, and re-layouts: 0.07 us -> 8.28 us
  transfers between devices with their start and end apart: 62 -> 0, of which waited for: 35 -> 0; matrix products, arithmetic and copies ran while one was open for 8% -> 0% of each run, Pallas kernels for 0% -> 0%
where the time goes in v1:
time: 68.2 us; the launch traced here: 67.8 us
  Pallas kernels  59.5 us (87%)
  local copies, waits for them, and re-layouts  8.28 us (12%)
    pallas_call x1, Pallas kernels, per_device(): pl.pallas_call(functools.partial(kernel, sizes, shape), out_shape=jax.Sha...  59.5 us
    unnamed x17, local copies, waits for them, and re-layouts  8.28 us

profile of v1, /device:TPU:0, one launch (start us, length us, event | category | flops | bytes accessed | tf_op | source)
XLA Modules:
  0.0 67.8 jit_solution(2701751960735132867)
XLA Ops:
  0.0 0.0 copy-start
  0.0 1.4 %copy-done = f32[2,2,128,768]{3,2,1,0:T(8,128)S(1)} copy-done((f32[2,2,128,768]{3,2,1,0:T(8,128)S(1)}, f32[2,2,128,768]{3,2,1,0:T(8,128)}, u32[]{:S(2)}) %copy-start) | copy-done | bytes 1572888
  1.4 0.0 copy-start.1
  1.4 1.0 %copy-done.1 = f32[32,32,128]{2,1,0:T(8,128)S(1)} copy-done((f32[32,32,128]{2,1,0:T(8,128)S(1)}, f32[32,32,128]{2,1,0:T(8,128)}, u32[]{:S(2)}) %copy-start.1) | copy-done | bytes 524312
  2.5 0.0 copy-start.2
  2.5 1.0 %copy-done.2 = s32[32,32,128]{2,1,0:T(8,128)S(1)} copy-done((s32[32,32,128]{2,1,0:T(8,128)S(1)}, s32[32,32,128]{2,1,0:T(8,128)}, u32[]{:S(2)}) %copy-start.2) | copy-done | bytes 524312
  3.5 0.0 copy-start.3
  3.5 1.0 %copy-done.3 = f32[2,2,256,128]{3,2,1,0:T(8,128)S(1)} copy-done((f32[2,2,256,128]{3,2,1,0:T(8,128)S(1)}, f32[2,2,256,128]{3,2,1,0:T(8,128)}, u32[]{:S(2)}) %copy-start.3) | copy-done | bytes 524312
  4.5 0.0 copy-start.4
  4.5 0.9 %copy-done.4 = f32[4,48,8]{2,1,0:T(8,128)S(1)} copy-done((f32[4,48,8]{2,1,0:T(8,128)S(1)}, f32[4,48,8]{2,1,0:T(8,128)}, u32[]{:S(2)}) %copy-start.4) | copy-done | bytes 6168
  5.4 0.0 copy-start.5
  5.4 0.7 %copy-done.5 = f32[4,8,32]{2,1,0:T(8,128)S(1)} copy-done((f32[4,8,32]{2,1,0:T(8,128)S(1)}, f32[4,8,32]{2,1,0:T(8,128)}, u32[]{:S(2)}) %copy-start.5) | copy-done | bytes 4120
  6.1 0.0 copy-start.6
  6.1 0.7 %copy-done.6 = f32[8,128]{1,0:T(8,128)S(1)} copy-done((f32[8,128]{1,0:T(8,128)S(1)}, f32[8,128]{1,0:T(8,128)}, u32[]{:S(2)}) %copy-start.6) | copy-done | bytes 4120
  6.8 0.0 copy-start.7
  6.8 0.7 copy-done.7
  7.5 59.5 %shard_map.82 = f32[32,32,128]{2,1,0:T(8,128)S(1)} custom-call(f32[32,32,128]{2,1,0:T(8,128)S(1)} %copy-done.1, s32[32,32,128]{2,1,0:T(8,128)S(1)} %copy-done.2, f32[8]{0:T(128)S(1)} %copy-done.7, f32[2,2,128,768]{3,2,1,0:T(8,128)S(1)} %copy-done, f32[2,2,256,128]{3,2,1,0:T(8,128)S(1)} %copy-done.3, f32[4,48,8]{2,1,0:T(8,128)S(1)} %copy-done.4, ...), custom_call_target="tpu_custom_call" | custom-call | tf_op jit(solution)/shard_map/pallas_call | solution.py:387
  67.0 0.8 %copy.10 = f32[32,32,128]{2,1,0:T(8,128)} copy(f32[32,32,128]{2,1,0:T(8,128)S(1)} %shard_map.82) | data formatting | bytes 1048576
Async XLA Ops:
  0.0 1.4 %copy-start = (f32[2,2,128,768]{3,2,1,0:T(8,128)S(1)}, f32[2,2,128,768]{3,2,1,0:T(8,128)}, u32[]{:S(2)}) copy-start(f32[2,2,128,768]{3,2,1,0:T(8,128)} %constant.10.clone.spread_hbm) | copy-start | bytes 4718596
  1.4 1.0 %copy-start.1 = (f32[32,32,128]{2,1,0:T(8,128)S(1)}, f32[32,32,128]{2,1,0:T(8,128)}, u32[]{:S(2)}) copy-start(f32[32,32,128]{2,1,0:T(8,128)} %heat.1) | copy-start | bytes 1572868
  2.5 1.0 %copy-start.2 = (s32[32,32,128]{2,1,0:T(8,128)S(1)}, s32[32,32,128]{2,1,0:T(8,128)}, u32[]{:S(2)}) copy-start(s32[32,32,128]{2,1,0:T(8,128)} %mat.1) | copy-start | bytes 1572868
  3.5 1.0 %copy-start.3 = (f32[2,2,256,128]{3,2,1,0:T(8,128)S(1)}, f32[2,2,256,128]{3,2,1,0:T(8,128)}, u32[]{:S(2)}) copy-start(f32[2,2,256,128]{3,2,1,0:T(8,128)} %constant.11.clone.gather_hbm) | copy-start | bytes 1572868
  4.5 0.9 %copy-start.4 = (f32[4,48,8]{2,1,0:T(8,128)S(1)}, f32[4,48,8]{2,1,0:T(8,128)}, u32[]{:S(2)}) copy-start(f32[4,48,8]{2,1,0:T(8,128)} %constant.12.clone.expand_hbm) | copy-start | bytes 18436
  5.4 0.7 %copy-start.5 = (f32[4,8,32]{2,1,0:T(8,128)S(1)}, f32[4,8,32]{2,1,0:T(8,128)}, u32[]{:S(2)}) copy-start(f32[4,8,32]{2,1,0:T(8,128)} %constant.13.clone.shrink_hbm) | copy-start | bytes 12292
  6.1 0.7 %copy-start.6 = (f32[8,128]{1,0:T(8,128)S(1)}, f32[8,128]{1,0:T(8,128)}, u32[]{:S(2)}) copy-start(f32[8,128]{1,0:T(8,128)} %constant.14.clone.scale) | copy-start | bytes 12292
  6.8 0.7 copy-start.7

commit v2 on v1

--- a/solution.py
+++ b/solution.py
@@ -11,9 +11,10 @@
 
 BLOCK = 16
 PAD = 8
+UNROLL = 4
 MESH = pl.DeviceIdType.MESH
 HIGH = lax.Precision.HIGHEST
-ROUNDS = 8
+ROUNDS = 9
 
 
 def sine_rows(count):
@@ -44,11 +45,11 @@
                 spread[a, b, :cols, i * 128 : i * 128 + shape[2]] = block
                 if 1 <= i <= lz:
                     gather[a, b, (i - 1) * 128 : i * 128, :cols] = block.T
-            fine = np.floor_divide(np.arange(shape[0]) + b * shape[0], BLOCK) + 1
+            fine = np.floor_divide(np.arange(0, shape[0], 2) + b * shape[0], BLOCK) + 1
             for side, row in ((0, yrow[0]), (1, yrow[-1])):
                 block = np.einsum("zp,q->pqz", sz[fine], sy[row]).reshape(cols, -1)
                 at = (lz + 2 + side) * 128
-                spread[a, b, :cols, at : at + shape[0]] = block
+                spread[a, b, :cols, at : at + shape[0] // 2] = block
     rows = shape[1] + 2 * PAD
     expand = np.zeros((n_gx, rows, fx))
     shrink = np.zeros((n_gx, fx, shape[1]))
@@ -65,13 +66,14 @@
 
 
 def kernel(
-    sizes, shape, heat, mat, table, spread_hbm, gather_hbm, expand_hbm, shrink_hbm, scale,
-    out, kp, u, wd, hd, dg, vsum, corr, spread, gather, expand, shrink,
-    s_z, r_z, s_x, r_x, s_y, r_y, got, tab_sem, send_sem, recv_sem, gsend, grecv,
+    sizes, shape, heat_hbm, mat_hbm, table_hbm, spread_hbm, gather_hbm, expand_hbm, shrink_hbm, scale_hbm,
+    out, heat, mat, table, kr, kb, red, black, wd, hd, dg, vsum, corr, spread, gather, expand, shrink,
+    scale, s_z, r_z, s_x, r_x, s_y, r_y, got, tab_sem, send_sem, recv_sem, gsend, grecv,
 ):
     n_gx, n_gy, n_gz = sizes
     nz, nx, ny = shape
     lz = nz // BLOCK
+    pairs = nz // 2
     rows = nx + 2 * PAD
     gx, gy, gz = lax.axis_index("gx"), lax.axis_index("gy"), lax.axis_index("gz")
     count = n_gx * n_gy * n_gz
@@ -85,6 +87,13 @@
             "gz": lax.rem(other, n_gz),
         }
 
+    inputs = [
+        pltpu.make_async_copy(table_hbm, table, tab_sem.at[5]),
+        pltpu.make_async_copy(mat_hbm, mat, tab_sem.at[6]),
+        pltpu.make_async_copy(heat_hbm, heat, tab_sem.at[7]),
+    ]
+    for copy in inputs:
+        copy.start()
     barrier = pltpu.get_barrier_semaphore()
 
     def greet(step, carry):
@@ -99,6 +108,7 @@
         pltpu.make_async_copy(gather_hbm.at[gy, gz], gather, tab_sem.at[1]),
         pltpu.make_async_copy(expand_hbm.at[gx], expand, tab_sem.at[2]),
         pltpu.make_async_copy(shrink_hbm.at[gx], shrink, tab_sem.at[3]),
+        pltpu.make_async_copy(scale_hbm, scale, tab_sem.at[4]),
     ]
     for copy in fetch:
         copy.start()
@@ -142,7 +152,7 @@
 
     lane = lax.broadcasted_iota(jnp.int32, (nx, ny), 1)
     row = lax.broadcasted_iota(jnp.int32, (nx, ny), 0)
-    odd = lax.rem(lane + row, 2)
+    even = lax.rem(lane + row, 2) == 0
     zero = jnp.zeros((nx, ny), jnp.float32)
     for buf, size, index in ((r_z, n_gz, gz), (r_x, n_gx, gx), (r_y, n_gy, gy)):
         if buf is r_y and single:
@@ -168,9 +178,9 @@
 
     def send(turn, field, packs):
         s_z[turn, 0] = field[pl.ds(rows + PAD, nx), :]
-        s_z[turn, 1] = field[pl.ds(nz * rows + PAD, nx), :]
+        s_z[turn, 1] = field[pl.ds(pairs * rows + PAD, nx), :]
         for side, at in ((0, PAD), (1, PAD + nx - 1)):
-            s_x[turn, side] = field[pl.ds(rows + at, nz, stride=rows), :]
+            s_x[turn, side] = field[pl.ds(rows + at, pairs, stride=rows), :]
         for side, pack in enumerate(packs):
             s_y[turn, side] = pack
         for exists, copy in copies(turn, False):
@@ -180,9 +190,9 @@
         for exists, copy in copies(turn, True):
             guarded(exists, copy.wait_recv)
         field[pl.ds(PAD, nx), :] = r_z[turn, 0]
-        field[pl.ds((nz + 1) * rows + PAD, nx), :] = r_z[turn, 1]
+        field[pl.ds((pairs + 1) * rows + PAD, nx), :] = r_z[turn, 1]
         for side, at in ((0, PAD - 1), (1, PAD + nx)):
-            field[pl.ds(rows + at, nz, stride=rows), :] = r_x[turn, side]
+            field[pl.ds(rows + at, pairs, stride=rows), :] = r_x[turn, side]
 
     def beside(value, halos, z, strict):
         low, high = pltpu.roll(value, 1, 1), pltpu.roll(value, ny - 1, 1)
@@ -201,13 +211,14 @@
         last = pltpu.roll(halos[1], lax.rem(2 * ny - 1 - z, ny), 1)
         return jnp.where(lane == 0, first, low), jnp.where(lane == ny - 1, last, high)
 
-    def around(field, halos, z, strict=False):
-        value = field[slab(z + 1), :]
-        low, high = beside(value, halos, z, strict)
+    def around(field, color, halos, z, strict=False):
+        same = field[slab(z + 1), :]
+        before, after = field[slab(z), :], field[slab(z + 2), :]
+        low, high = beside(same, halos, z, strict)
         at = pl.multiple_of((z + 1) * rows, 8) + PAD
-        return value, (
-            field[slab(z), :],
-            field[slab(z + 2), :],
+        return (
+            same,
+            jnp.where(even, before, after) if color == 0 else jnp.where(even, after, before),
             field[pl.ds(at - 1, nx), :],
             field[pl.ds(at + 1, nx), :],
             low,
@@ -217,76 +228,96 @@
     def y_halos(turn):
         return [r_y[turn, side] for side in range(len(edges))]
 
+    def loop(count, step, carry, start=0):
+        return lax.fori_loop(start, count, step, carry, unroll=UNROLL)
+
     def conduct(z, packs):
-        ids = mat[z]
-        value = jnp.full((nx, ny), table[0], jnp.float32)
-        for m in range(1, table.shape[0]):
-            value = jnp.where(ids == m, table[m], value)
-        kp[slab(z + 1), :] = value
-        return packed(packs, value, z)
-
-    packs = lax.fori_loop(0, nz, conduct, blank, unroll=2)
+        values = []
+        for layer in range(2):
+            ids = mat[2 * z + layer]
+            value = jnp.full((nx, ny), table[0], jnp.float32)
+            for m in range(1, table.shape[0]):
+                value = jnp.where(ids == m, table[m], value)
+            values.append(value)
+        first = jnp.where(even, values[0], values[1])
+        second = jnp.where(even, values[1], values[0])
+        kr[slab(z + 1), :] = first
+        kb[slab(z + 1), :] = second
+        return packed(packs[0], first, z), packed(packs[1], second, z)
+
+    inputs[0].wait()
+    inputs[1].wait()
+    packs = loop(pairs, conduct, (blank, blank))
     pl.semaphore_wait(barrier, count - 1)
-    send(0, kp, packs)
-    receive(0, kp)
-    halos = y_halos(0)
-
-    def weigh(z, packs):
-        center, others = around(kp, halos, z, True)
-        diag = None
-        inner = []
-        for other in others:
-            inside = other > 0.0
-            weight = 2.0 * center * other / (center + other)
-            full = jnp.where(inside, weight, center)
-            inner.append(jnp.where(inside, weight, 0.0))
-            diag = full if diag is None else diag + full
-        inverse = 1.0 / diag
+    send(0, kr, packs[0])
+    send(1, kb, packs[1])
+    inputs[2].wait()
+    receive(0, kr)
+    receive(1, kb)
+
+    def weigh(color, own, field, turn, first):
+        halos = y_halos(turn)
+
+        def step(z, packs):
+            center = own[slab(z + 1), :]
+            others = around(field, color, halos, z, True)
+            diag = None
+            inner = []
+            for other in others:
+                inside = other > 0.0
+                weight = 2.0 * center * other / (center + other)
+                full = jnp.where(inside, weight, center)
+                inner.append(jnp.where(inside, weight, 0.0))
+                diag = full if diag is None else diag + full
+            inverse = 1.0 / diag
+            for face in range(6):
+                wd[color, face, z] = inner[face] * inverse
+            lower, upper = heat[2 * z], heat[2 * z + 1]
+            source = jnp.where(even, lower, upper) if color == 0 else jnp.where(even, upper, lower)
+            ratio = source * inverse
+            hd[color, z] = ratio
+            if not first:
+                return packs
+            dg[z] = diag
+            red[slab(z + 1), :] = ratio
+            return packed(packs, ratio, z)
+
+        return loop(pairs, step, blank if first else 0)
+
+    packs = weigh(0, kr, kb, 1, True)
+    send(2, red, packs)
+    weigh(1, kb, kr, 0, False)
+
+    def total(color, field, halos, z):
+        others = around(field, color, halos, z)
+        result = hd[color, z]
         for face in range(6):
-            wd[face, z] = inner[face] * inverse
-        ratio = heat[z] * inverse
-        hd[z] = ratio
-        dg[z] = diag
-        value = jnp.where(odd == lax.rem(z, 2), ratio, 0.0)
-        u[slab(z + 1), :] = value
-        return packed(packs, value, z)
-
-    packs = lax.fori_loop(0, nz, weigh, blank)
-    send(1, u, packs)
-
-    def total(z, halos):
-        value, others = around(u, halos, z)
-        result = hd[z]
-        for face in range(6):
-            result = result + wd[face, z] * others[face]
-        return value, result
-
-    def half(color, halos, last=False):
+            result = result + wd[color, face, z] * others[face]
+        return result
+
+    def half(color, halos):
+        field, own = ((black, red), (red, black))[color]
+
         def step(z, packs):
-            value, result = total(z, halos)
-            value = jnp.where(odd == lax.rem(z + color, 2), result, value)
-            if last:
-                out[z] = value
-                return packs
-            u[slab(z + 1), :] = value
+            value = total(color, field, halos, z)
+            own[slab(z + 1), :] = value
             return packed(packs, value, z)
 
-        return lax.fori_loop(0, nz, step, blank, unroll=2)
-
-    for turn, color in ((2, 1), (3, 0), (4, 1)):
-        receive(turn - 1, u)
+        return loop(pairs, step, blank)
+
+    for turn, color in ((3, 1), (4, 0), (5, 1)):
+        receive(turn - 1, (black, red)[color])
         packs = half(color, y_halos(turn - 1))
-        send(turn, u, packs)
-    receive(4, u)
-    halos = y_halos(4)
+        send(turn, (red, black)[color], packs)
+    receive(5, black)
+    halos = y_halos(5)
 
     for layer in range(lz):
         def gap(z, acc):
-            value, result = total(z, halos)
-            return acc + jnp.where(odd == lax.rem(z, 2), dg[z] * (result - value), 0.0)
-
-        vsum[:, layer * ny : (layer + 1) * ny] = lax.fori_loop(
-            layer * BLOCK, (layer + 1) * BLOCK, gap, zero, unroll=2
+            return acc + dg[z] * (total(0, black, halos, z) - red[slab(z + 1), :])
+
+        vsum[:, layer * ny : (layer + 1) * ny] = loop(
+            (layer + 1) * BLOCK // 2, gap, zero, layer * BLOCK // 2
         )
     for copy in fetch:
         copy.wait()
@@ -331,12 +362,12 @@
     corr[...] = jnp.dot(expand[...], hat, precision=HIGH, preferred_element_type=jnp.float32)
 
     def correct(z, carry):
-        layer = (z + BLOCK - 1) // BLOCK
+        layer = (z + BLOCK // 2 - 1) // (BLOCK // 2)
         at = pl.ds(pl.multiple_of(z * rows, 8), rows)
-        u[at, :] = u[at, :] + corr[:, pl.ds(pl.multiple_of(layer * ny, ny), ny)]
-        return carry
-
-    lax.fori_loop(0, nz + 2, correct, 0, unroll=2)
+        black[at, :] = black[at, :] + corr[:, pl.ds(pl.multiple_of(layer * ny, ny), ny)]
+        return carry
+
+    lax.fori_loop(0, pairs + 2, correct, 0, unroll=2)
     sides = [corr[PAD : PAD + nx, (lz + 2 + s) * ny : (lz + 3 + s) * ny] for s in range(2)]
     if single:
         upper = gy.astype(jnp.float32)
@@ -345,13 +376,22 @@
         halos = [halo + side for halo, side in zip(halos, sides)]
 
     packs = half(0, halos)
-    send(5, u, packs)
-    for turn, color in ((6, 1), (7, 0)):
-        receive(turn - 1, u)
+    send(6, red, packs)
+    for turn, color in ((7, 1), (8, 0)):
+        receive(turn - 1, (black, red)[color])
         packs = half(color, y_halos(turn - 1))
-        send(turn, u, packs)
-    receive(7, u)
-    half(1, y_halos(7), True)
+        send(turn, (red, black)[color], packs)
+    receive(8, red)
+    halos = y_halos(8)
+
+    def finish(z, carry):
+        last = total(1, red, halos, z)
+        own = red[slab(z + 1), :]
+        out[2 * z] = jnp.where(even, own, last)
+        out[2 * z + 1] = jnp.where(even, last, own)
+        return carry
+
+    loop(pairs, finish, 0)
 
     for turn in range(ROUNDS):
         for exists, copy in copies(turn, False):
@@ -375,42 +415,45 @@
     sides = 1 if n_gy == 2 else 2
     f32 = jnp.float32
     vmem = pl.BlockSpec(memory_space=pltpu.VMEM)
-    hbm = pl.BlockSpec(memory_space=pl.ANY)
+    hbm = pl.BlockSpec(memory_space=pltpu.HBM)
     faces = [
         pltpu.VMEM((ROUNDS, 2, nx, ny), f32),
         pltpu.VMEM((ROUNDS, 2, nx, ny), f32),
-        pltpu.VMEM((ROUNDS, 2, nz, ny), f32),
-        pltpu.VMEM((ROUNDS, 2, nz, ny), f32),
+        pltpu.VMEM((ROUNDS, 2, nz // 2, ny), f32),
+        pltpu.VMEM((ROUNDS, 2, nz // 2, ny), f32),
         pltpu.VMEM((ROUNDS, sides, nx, ny), f32),
         pltpu.VMEM((ROUNDS, sides, nx, ny), f32),
     ]
     return pl.pallas_call(
         functools.partial(kernel, sizes, shape),
         out_shape=jax.ShapeDtypeStruct(shape, f32),
-        in_specs=[vmem, vmem, pl.BlockSpec(memory_space=pltpu.SMEM), hbm, hbm, hbm, hbm, vmem],
+        in_specs=[hbm] * 8,
         out_specs=vmem,
         scratch_shapes=[
-            pltpu.VMEM(((nz + 2) * rows, ny), f32),
-            pltpu.VMEM(((nz + 2) * rows, ny), f32),
-            pltpu.VMEM((6, nz, nx, ny), f32),
             pltpu.VMEM(shape, f32),
-            pltpu.VMEM(shape, f32),
+            pltpu.VMEM(shape, jnp.int32),
+            pltpu.SMEM(table.shape, f32),
+            *[pltpu.VMEM(((nz // 2 + 2) * rows, ny), f32)] * 4,
+            pltpu.VMEM((2, 6, nz // 2, nx, ny), f32),
+            pltpu.VMEM((2, nz // 2, nx, ny), f32),
+            pltpu.VMEM((nz // 2, nx, ny), f32),
             pltpu.VMEM((nx, nz // BLOCK * ny), f32),
             pltpu.VMEM((rows, spread.shape[3]), f32),
             pltpu.VMEM(spread.shape[2:], f32),
             pltpu.VMEM(gather.shape[2:], f32),
             pltpu.VMEM(expand.shape[1:], f32),
             pltpu.VMEM(shrink.shape[1:], f32),
+            pltpu.VMEM(scale.shape, f32),
             *faces,
             pltpu.VMEM((count, *scale.shape), f32),
-            pltpu.SemaphoreType.DMA((4,)),
+            pltpu.SemaphoreType.DMA((8,)),
             pltpu.SemaphoreType.DMA((ROUNDS, 6)),
             pltpu.SemaphoreType.DMA((ROUNDS, 6)),
             pltpu.SemaphoreType.DMA((count,)),
             pltpu.SemaphoreType.DMA((count,)),
         ],
         compiler_params=pltpu.CompilerParams(
-            collective_id=0, has_side_effects=True, vmem_limit_bytes=50 * 1024 * 1024
+            collective_id=0, has_side_effects=True, vmem_limit_bytes=64 * 1024 * 1024
         ),
     )(heat, material, table, *(jnp.asarray(c) for c in consts))
 

time: 68.2 us -> 44.1 us (0.65)
  Pallas kernels: 59.5 us -> 42 us
  local copies, waits for them, and re-layouts: 8.28 us -> 1.87 us
    pallas_call x1, Pallas kernels: 59.5 us -> 42 us  [per_device(): pl.pallas_call(functools.partial(kernel, sizes, shape), out_shape=jax.Sha...]
    unnamed x17 -> x1, local copies, waits for them, and re-layouts: 8.28 us -> 1.87 us
where the time goes in v2:
time: 44.1 us; the launch traced here: 43.9 us
  Pallas kernels  42 us (95%)
  local copies, waits for them, and re-layouts  1.87 us (4%)
    pallas_call x1, Pallas kernels, per_device(): pl.pallas_call(functools.partial(kernel, sizes, shape), out_shape=jax.Sha...  42 us
    unnamed x1, local copies, waits for them, and re-layouts  1.87 us

profile of v2, /device:TPU:0, one launch (start us, length us, event | category | flops | bytes accessed | tf_op | source)
XLA Modules:
  0.0 43.9 jit_solution(1000113848850616367)
XLA Ops:
  0.0 42.0 %shard_map.82 = f32[32,32,128]{2,1,0:T(8,128)} custom-call(f32[32,32,128]{2,1,0:T(8,128)} %heat_hbm.1, s32[32,32,128]{2,1,0:T(8,128)} %mat_hbm.1, f32[8]{0:T(128)} %table_hbm.1, f32[2,2,128,768]{3,2,1,0:T(8,128)} %constant.10.clone.spread_hbm, f32[2,2,256,128]{3,2,1,0:T(8,128)} %constant.11.clone.gather_hbm, f32[4,48,8]{2,1,0:T(8,128)} %constant.12.clone.expand_hbm, ...), custom_call_target="tpu_custom_call" | custom-call | tf_op jit(solution)/shard_map/pallas_call | solution.py:427
  42.0 1.9 %copy.10 = f32[32,32,128]{2,1,0:T(8,128)} copy(f32[32,32,128]{2,1,0:T(8,128)} %shard_map.82) | data formatting | bytes 1048576

commit v3 on v2

--- a/solution.py
+++ b/solution.py
@@ -11,7 +11,7 @@
 
 BLOCK = 16
 PAD = 8
-UNROLL = 4
+UNROLL = 8
 MESH = pl.DeviceIdType.MESH
 HIGH = lax.Precision.HIGHEST
 ROUNDS = 9
@@ -35,7 +35,7 @@
     zs = np.arange(-1, shape[0] + 1)
     ys = np.arange(-1, shape[2] + 1)
     spread = np.zeros((n_gy, n_gz, wide, (lz + 4) * 128))
-    gather = np.zeros((n_gy, n_gz, lz * 128, wide))
+    gather = np.zeros((n_gy, n_gz, (2 * lz + 2) * 128, wide))
     for a in range(n_gy):
         yrow = np.floor_divide(ys + a * shape[2], BLOCK) + 1
         for b in range(n_gz):
@@ -43,8 +43,11 @@
             for i, row in enumerate(zrow):
                 block = np.einsum("p,yq->pqy", sz[row], sy[yrow[1:-1]]).reshape(cols, -1)
                 spread[a, b, :cols, i * 128 : i * 128 + shape[2]] = block
+                gather[a, b, i * 128 : i * 128 + shape[2], :cols] = block.T
                 if 1 <= i <= lz:
-                    gather[a, b, (i - 1) * 128 : i * 128, :cols] = block.T
+                    at = (lz + 1 + i) * 128
+                    gather[a, b, at, :cols] = np.outer(sz[row], sy[yrow[0]]).reshape(-1)
+                    gather[a, b, at + shape[2] - 1, :cols] = np.outer(sz[row], sy[yrow[-1]]).reshape(-1)
             fine = np.floor_divide(np.arange(0, shape[0], 2) + b * shape[0], BLOCK) + 1
             for side, row in ((0, yrow[0]), (1, yrow[-1])):
                 block = np.einsum("zp,q->pqz", sz[fine], sy[row]).reshape(cols, -1)
@@ -52,12 +55,11 @@
                 spread[a, b, :cols, at : at + shape[0] // 2] = block
     rows = shape[1] + 2 * PAD
     expand = np.zeros((n_gx, rows, fx))
-    shrink = np.zeros((n_gx, fx, shape[1]))
     for a in range(n_gx):
         xs = np.arange(-1, shape[1] + 1) + a * shape[1]
         block = sx[np.floor_divide(xs, BLOCK) + 1]
         expand[a, PAD - 1 : PAD + shape[1] + 1] = block
-        shrink[a] = block[1:-1].T
+    shrink = expand.transpose(0, 2, 1)
     lam = lambda n: 2.0 - 2.0 * np.cos(math.pi * (np.arange(n) + 1.0) / (n + 1))
     total = lam(fx)[:, None] + (lam(fz)[:, None] + lam(fy)[None, :]).reshape(1, -1)
     scale = np.zeros((fx, wide))
@@ -276,9 +278,9 @@
             source = jnp.where(even, lower, upper) if color == 0 else jnp.where(even, upper, lower)
             ratio = source * inverse
             hd[color, z] = ratio
+            dg[color, z] = diag
             if not first:
                 return packs
-            dg[z] = diag
             red[slab(z + 1), :] = ratio
             return packed(packs, ratio, z)
 
@@ -309,16 +311,40 @@
         receive(turn - 1, (black, red)[color])
         packs = half(color, y_halos(turn - 1))
         send(turn, (red, black)[color], packs)
-    receive(5, black)
-    halos = y_halos(5)
+
+    black[pl.ds(PAD, nx), :] = zero
+    black[pl.ds((pairs + 1) * rows + PAD, nx), :] = zero
+    for at in (PAD - 1, PAD + nx):
+        black[pl.ds(rows + at, pairs, stride=rows), :] = jnp.zeros((pairs, ny), jnp.float32)
+    vsum[...] = jnp.zeros(vsum.shape, jnp.float32)
+    tile = jnp.zeros((8, ny), jnp.float32)
+    tile_row = lax.broadcasted_iota(jnp.int32, (8, ny), 0)
+
+    def outward(z):
+        return dg[1, z] * black[slab(z + 1), :]
 
     for layer in range(lz):
-        def gap(z, acc):
-            return acc + dg[z] * (total(0, black, halos, z) - red[slab(z + 1), :])
-
-        vsum[:, layer * ny : (layer + 1) * ny] = loop(
-            (layer + 1) * BLOCK // 2, gap, zero, layer * BLOCK // 2
+        def gap(z, sums):
+            inner, low, high, ends = sums
+            flow = outward(z)
+            inner = inner + dg[0, z] * (total(0, black, blank, z) - red[slab(z + 1), :])
+            low = low + (wd[1, 2, z] * flow)[:8]
+            high = high + (wd[1, 3, z] * flow)[nx - 8 :]
+            weight = jnp.where(lane == 0, wd[1, 4, z], jnp.where(lane == ny - 1, wd[1, 5, z], 0.0))
+            return inner, low, high, ends + weight * flow
+
+        inner, low, high, ends = loop(
+            (layer + 1) * BLOCK // 2, gap, (zero, tile, tile, zero), layer * BLOCK // 2
         )
+        here = slice((layer + 1) * ny, (layer + 2) * ny)
+        vsum[PAD : PAD + nx, here] = inner
+        vsum[PAD - 8 : PAD, here] = jnp.where(tile_row == 7, pltpu.roll(low, 7, 0), 0.0)
+        vsum[PAD + nx : PAD + nx + 8, here] = jnp.where(tile_row == 0, pltpu.roll(high, 1, 0), 0.0)
+        vsum[PAD : PAD + nx, (lz + 2 + layer) * ny : (lz + 3 + layer) * ny] = ends
+    vsum[PAD : PAD + nx, :ny] = jnp.where(even, 0.0, wd[1, 1, 0] * outward(0))
+    vsum[PAD : PAD + nx, (lz + 1) * ny : (lz + 2) * ny] = jnp.where(
+        even, wd[1, 1, pairs - 1] * outward(pairs - 1), 0.0
+    )
     for copy in fetch:
         copy.wait()
     part = jnp.dot(shrink[...], vsum[...], precision=HIGH, preferred_element_type=jnp.float32)
@@ -346,6 +372,8 @@
         return carry
 
     lax.fori_loop(1, count, give, 0)
+    receive(5, black)
+    halos = y_halos(5)
     lax.fori_loop(1, count, take, 0)
     if count <= 32:
         hat = got[0]
@@ -436,8 +464,8 @@
             *[pltpu.VMEM(((nz // 2 + 2) * rows, ny), f32)] * 4,
             pltpu.VMEM((2, 6, nz // 2, nx, ny), f32),
             pltpu.VMEM((2, nz // 2, nx, ny), f32),
-            pltpu.VMEM((nz // 2, nx, ny), f32),
-            pltpu.VMEM((nx, nz // BLOCK * ny), f32),
+            pltpu.VMEM((2, nz // 2, nx, ny), f32),
+            pltpu.VMEM((rows, gather.shape[2]), f32),
             pltpu.VMEM((rows, spread.shape[3]), f32),
             pltpu.VMEM(spread.shape[2:], f32),
             pltpu.VMEM(gather.shape[2:], f32),

time: 44.1 us -> 39.5 us (0.90)
  Pallas kernels: 42 us -> 37.5 us
    pallas_call x1, Pallas kernels: 42 us -> 37.5 us  [per_device(): pl.pallas_call(functools.partial(kernel, sizes, shape), out_shape=jax.Sha...]
where the time goes in v3:
time: 39.5 us; the launch traced here: 39.4 us
  Pallas kernels  37.5 us (95%)
  local copies, waits for them, and re-layouts  1.87 us (5%)
    pallas_call x1, Pallas kernels, per_device(): pl.pallas_call(functools.partial(kernel, sizes, shape), out_shape=jax.Sha...  37.5 us
    unnamed x1, local copies, waits for them, and re-layouts  1.87 us

profile of v3, /device:TPU:0, one launch (start us, length us, event | category | flops | bytes accessed | tf_op | source)
XLA Modules:
  0.0 39.4 jit_solution(2014725316473052105)
XLA Ops:
  0.0 37.5 %shard_map.82 = f32[32,32,128]{2,1,0:T(8,128)} custom-call(f32[32,32,128]{2,1,0:T(8,128)} %heat_hbm.1, s32[32,32,128]{2,1,0:T(8,128)} %mat_hbm.1, f32[8]{0:T(128)} %table_hbm.1, f32[2,2,128,768]{3,2,1,0:T(8,128)} %constant.10.clone.spread_hbm, f32[2,2,768,128]{3,2,1,0:T(8,128)} %constant.11.clone.gather_hbm, f32[4,48,8]{2,1,0:T(8,128)} %constant.12.clone.expand_hbm, ...), custom_call_target="tpu_custom_call" | custom-call | tf_op jit(solution)/shard_map/pallas_call | solution.py:455
  37.5 1.9 %copy.10 = f32[32,32,128]{2,1,0:T(8,128)} copy(f32[32,32,128]{2,1,0:T(8,128)} %shard_map.82) | data formatting | bytes 1048576

commit v4 on v3

--- a/solution.py
+++ b/solution.py
@@ -69,7 +69,7 @@
 
 def kernel(
     sizes, shape, heat_hbm, mat_hbm, table_hbm, spread_hbm, gather_hbm, expand_hbm, shrink_hbm, scale_hbm,
-    out, heat, mat, table, kr, kb, red, black, wd, hd, dg, vsum, corr, spread, gather, expand, shrink,
+    out, heat, mat, table, kr, kb, red, black, ahead, wd, wxf, wyf, hd, dg, vsum, corr, spread, gather, expand, shrink,
     scale, s_z, r_z, s_x, r_x, s_y, r_y, got, tab_sem, send_sem, recv_sem, gsend, grecv,
 ):
     n_gx, n_gy, n_gz = sizes
@@ -81,13 +81,39 @@
     count = n_gx * n_gy * n_gz
     me = (gx * n_gy + gy) * n_gz + gz
 
+    few = count <= 32
+    offsets = sorted(
+        ((a, b, c) for a in range(n_gx) for b in range(n_gy) for c in range(n_gz) if a or b or c),
+        key=lambda o: (-min(o[0], n_gx - o[0]), -min(o[1], n_gy - o[1]), -o[2]),
+    )
+
+    def turned(position, step, size):
+        at = position + step
+        return jnp.where(at >= size, at - size, at)
+
     def peer_of(step):
+        if few:
+            a, b, c = offsets[step - 1]
+            at = turned(gx, a, n_gx), turned(gy, b, n_gy), turned(gz, c, n_gz)
+            return (at[0] * n_gy + at[1]) * n_gz + at[2], dict(zip(("gx", "gy", "gz"), at))
         other = lax.rem(me + step, count)
         return other, {
             "gx": other // (n_gy * n_gz),
             "gy": lax.rem(other // n_gz, n_gy),
             "gz": lax.rem(other, n_gz),
         }
+
+    def each_peer(action):
+        if few:
+            for step in range(1, count):
+                action(step)
+            return
+
+        def one(step, carry):
+            action(step)
+            return carry
+
+        lax.fori_loop(1, count, one, 0)
 
     inputs = [
         pltpu.make_async_copy(table_hbm, table, tab_sem.at[5]),
@@ -98,12 +124,11 @@
         copy.start()
     barrier = pltpu.get_barrier_semaphore()
 
-    def greet(step, carry):
+    def greet(step):
         _, where = peer_of(step)
         pl.semaphore_signal(barrier, inc=1, device_id=where, device_id_type=MESH)
-        return carry
-
-    lax.fori_loop(1, count, greet, 0)
+
+    each_peer(greet)
 
     fetch = [
         pltpu.make_async_copy(spread_hbm.at[gy, gz], spread, tab_sem.at[0]),
@@ -257,10 +282,17 @@
     receive(0, kr)
     receive(1, kb)
 
+    def quiet(field):
+        field[pl.ds(PAD, nx), :] = zero
+        field[pl.ds((pairs + 1) * rows + PAD, nx), :] = zero
+        for at in (PAD - 1, PAD + nx):
+            field[pl.ds(rows + at, pairs, stride=rows), :] = jnp.zeros((pairs, ny), jnp.float32)
+
     def weigh(color, own, field, turn, first):
         halos = y_halos(turn)
 
-        def step(z, packs):
+        def step(z, carry):
+            packs, edge_packs = carry
             center = own[slab(z + 1), :]
             others = around(field, color, halos, z, True)
             diag = None
@@ -273,19 +305,27 @@
                 diag = full if diag is None else diag + full
             inverse = 1.0 / diag
             for face in range(6):
-                wd[color, face, z] = inner[face] * inverse
+                inner[face] = inner[face] * inverse
+                wd[color, face, z] = inner[face]
+            wxf[color, 0, pl.ds(z, 1), :] = inner[2][:1]
+            wxf[color, 1, pl.ds(z, 1), :] = inner[3][nx - 1 :]
+            edge_packs = packed(edge_packs, jnp.where(lane == 0, inner[4], inner[5]), z)
             lower, upper = heat[2 * z], heat[2 * z + 1]
             source = jnp.where(even, lower, upper) if color == 0 else jnp.where(even, upper, lower)
             ratio = source * inverse
             hd[color, z] = ratio
             dg[color, z] = diag
             if not first:
-                return packs
+                return packs, edge_packs
             red[slab(z + 1), :] = ratio
-            return packed(packs, ratio, z)
-
-        return loop(pairs, step, blank if first else 0)
-
+            return packed(packs, ratio, z), edge_packs
+
+        packs, edge_packs = loop(pairs, step, (blank, blank))
+        for side, pack in enumerate(edge_packs):
+            wyf[color, side] = pack
+        return packs
+
+    quiet(red)
     packs = weigh(0, kr, kb, 1, True)
     send(2, red, packs)
     weigh(1, kb, kr, 0, False)
@@ -297,25 +337,51 @@
             result = result + wd[color, face, z] * others[face]
         return result
 
-    def half(color, halos):
-        field, own = ((black, red), (red, black))[color]
-
-        def step(z, packs):
-            value = total(color, field, halos, z)
+    def early(color, halos=blank):
+        field = (black, red)[color]
+
+        def step(z, carry):
+            ahead[slab(z + 1), :] = total(color, field, halos, z)
+            return carry
+
+        loop(pairs, step, 0)
+
+    def late(turn, color, store, carry):
+        for exists, copy in copies(turn, True):
+            guarded(exists, copy.wait_recv)
+        for side, z in ((0, 0), (1, pairs - 1)):
+            term = wd[color, 1, z] * r_z[turn, side]
+            mine = even if side == color else jnp.logical_not(even)
+            ahead[slab(z + 1), :] = ahead[slab(z + 1), :] + jnp.where(mine, term, 0.0)
+        for side, at in ((0, PAD), (1, PAD + nx - 1)):
+            where = pl.ds(rows + at, pairs, stride=rows)
+            ahead[where, :] = ahead[where, :] + wxf[color, side] * r_x[turn, side]
+        terms = [wyf[color, side] * r_y[turn, side] for side in range(len(edges))]
+
+        def step(z, carry):
+            value = ahead[slab(z + 1), :]
+            for term, at in zip(terms, edges):
+                term = pltpu.roll(term, lax.rem(at - z + ny, ny), 1)
+                value = jnp.where(lane == at, value + term, value)
+            return store(z, value, carry)
+
+        return loop(pairs, step, carry)
+
+    def finished(turn, color):
+        own = (red, black)[color]
+
+        def store(z, value, packs):
             own[slab(z + 1), :] = value
             return packed(packs, value, z)
 
-        return loop(pairs, step, blank)
-
+        return late(turn, color, store, blank)
+
+    quiet(black)
     for turn, color in ((3, 1), (4, 0), (5, 1)):
-        receive(turn - 1, (black, red)[color])
-        packs = half(color, y_halos(turn - 1))
+        early(color)
+        packs = finished(turn - 1, color)
         send(turn, (red, black)[color], packs)
 
-    black[pl.ds(PAD, nx), :] = zero
-    black[pl.ds((pairs + 1) * rows + PAD, nx), :] = zero
-    for at in (PAD - 1, PAD + nx):
-        black[pl.ds(rows + at, pairs, stride=rows), :] = jnp.zeros((pairs, ny), jnp.float32)
     vsum[...] = jnp.zeros(vsum.shape, jnp.float32)
     tile = jnp.zeros((8, ny), jnp.float32)
     tile_row = lax.broadcasted_iota(jnp.int32, (8, ny), 0)
@@ -363,18 +429,8 @@
         )
         return copy
 
-    def give(step, carry):
-        gathering(step, True).start()
-        return carry
-
-    def take(step, carry):
-        gathering(step, False).wait_recv()
-        return carry
-
-    lax.fori_loop(1, count, give, 0)
-    receive(5, black)
-    halos = y_halos(5)
-    lax.fori_loop(1, count, take, 0)
+    each_peer(lambda step: gathering(step, True).start())
+    each_peer(lambda step: gathering(step, False).wait_recv())
     if count <= 32:
         hat = got[0]
         for i in range(1, count):
@@ -399,37 +455,30 @@
     sides = [corr[PAD : PAD + nx, (lz + 2 + s) * ny : (lz + 3 + s) * ny] for s in range(2)]
     if single:
         upper = gy.astype(jnp.float32)
-        halos = [halos[0] + sides[0] * upper + sides[1] * (1.0 - upper)]
-    else:
-        halos = [halo + side for halo, side in zip(halos, sides)]
-
-    packs = half(0, halos)
+        sides = [sides[0] * upper + sides[1] * (1.0 - upper)]
+    early(0, sides)
+    quiet(black)
+    packs = finished(5, 0)
     send(6, red, packs)
     for turn, color in ((7, 1), (8, 0)):
-        receive(turn - 1, (black, red)[color])
-        packs = half(color, y_halos(turn - 1))
+        early(color)
+        packs = finished(turn - 1, color)
         send(turn, (red, black)[color], packs)
-    receive(8, red)
-    halos = y_halos(8)
-
-    def finish(z, carry):
-        last = total(1, red, halos, z)
+    early(1)
+
+    def finish(z, last, carry):
         own = red[slab(z + 1), :]
         out[2 * z] = jnp.where(even, own, last)
         out[2 * z + 1] = jnp.where(even, last, own)
         return carry
 
-    loop(pairs, finish, 0)
+    late(8, 1, finish, 0)
 
     for turn in range(ROUNDS):
         for exists, copy in copies(turn, False):
             guarded(exists, copy.wait_send)
 
-    def sent(step, carry):
-        gathering(step, True).wait_send()
-        return carry
-
-    lax.fori_loop(1, count, sent, 0)
+    each_peer(lambda step: gathering(step, True).wait_send())
 
 
 def per_device(sizes, heat, material, table):
@@ -461,8 +510,10 @@
             pltpu.VMEM(shape, f32),
             pltpu.VMEM(shape, jnp.int32),
             pltpu.SMEM(table.shape, f32),
-            *[pltpu.VMEM(((nz // 2 + 2) * rows, ny), f32)] * 4,
+            *[pltpu.VMEM(((nz // 2 + 2) * rows, ny), f32)] * 5,
             pltpu.VMEM((2, 6, nz // 2, nx, ny), f32),
+            pltpu.VMEM((2, 2, nz // 2, ny), f32),
+            pltpu.VMEM((2, sides, nx, ny), f32),
             pltpu.VMEM((2, nz // 2, nx, ny), f32),
             pltpu.VMEM((2, nz // 2, nx, ny), f32),
             pltpu.VMEM((rows, gather.shape[2]), f32),

time: 39.5 us -> 38.4 us (0.972)
  Pallas kernels: 37.5 us -> 36.3 us
    pallas_call x1, Pallas kernels: 37.5 us -> 36.3 us  [per_device(): pl.pallas_call(functools.partial(kernel, sizes, shape), out_shape=jax.Sha...]
where the time goes in v4:
time: 38.4 us; the launch traced here: 38.2 us
  Pallas kernels  36.3 us (95%)
  local copies, waits for them, and re-layouts  1.87 us (5%)
    pallas_call x1, Pallas kernels, per_device(): pl.pallas_call(functools.partial(kernel, sizes, shape), out_shape=jax.Sha...  36.3 us
    unnamed x1, local copies, waits for them, and re-layouts  1.87 us

profile of v4, /device:TPU:0, one launch (start us, length us, event | category | flops | bytes accessed | tf_op | source)
XLA Modules:
  0.0 38.2 jit_solution(9494431200388823679)
XLA Ops:
  0.0 36.3 %shard_map.82 = f32[32,32,128]{2,1,0:T(8,128)} custom-call(f32[32,32,128]{2,1,0:T(8,128)} %heat_hbm.1, s32[32,32,128]{2,1,0:T(8,128)} %mat_hbm.1, f32[8]{0:T(128)} %table_hbm.1, f32[2,2,128,768]{3,2,1,0:T(8,128)} %constant.10.clone.spread_hbm, f32[2,2,768,128]{3,2,1,0:T(8,128)} %constant.11.clone.gather_hbm, f32[4,48,8]{2,1,0:T(8,128)} %constant.12.clone.expand_hbm, ...), custom_call_target="tpu_custom_call" | custom-call | tf_op jit(solution)/shard_map/pallas_call | solution.py:504
  36.3 1.9 %copy.10 = f32[32,32,128]{2,1,0:T(8,128)} copy(f32[32,32,128]{2,1,0:T(8,128)} %shard_map.82) | data formatting | bytes 1048576

commit v5 on v4

--- a/solution.py
+++ b/solution.py
@@ -365,7 +365,7 @@
                 value = jnp.where(lane == at, value + term, value)
             return store(z, value, carry)
 
-        return loop(pairs, step, carry)
+        return lax.fori_loop(0, pairs, step, carry, unroll=2 * UNROLL)
 
     def finished(turn, color):
         own = (red, black)[color]

time: 38.4 us -> 37.9 us (0.987)
  Pallas kernels: 36.3 us -> 35.9 us
    pallas_call x1, Pallas kernels: 36.3 us -> 35.9 us  [per_device(): pl.pallas_call(functools.partial(kernel, sizes, shape), out_shape=jax.Sha...]
where the time goes in v5:
time: 37.9 us; the launch traced here: 37.7 us
  Pallas kernels  35.9 us (95%)
  local copies, waits for them, and re-layouts  1.87 us (5%)
    pallas_call x1, Pallas kernels, per_device(): pl.pallas_call(functools.partial(kernel, sizes, shape), out_shape=jax.Sha...  35.9 us
    unnamed x1, local copies, waits for them, and re-layouts  1.87 us

profile of v5, /device:TPU:0, one launch (start us, length us, event | category | flops | bytes accessed | tf_op | source)
XLA Modules:
  0.0 37.7 jit_solution(3873025707426292723)
XLA Ops:
  0.0 35.9 %shard_map.82 = f32[32,32,128]{2,1,0:T(8,128)} custom-call(f32[32,32,128]{2,1,0:T(8,128)} %heat_hbm.1, s32[32,32,128]{2,1,0:T(8,128)} %mat_hbm.1, f32[8]{0:T(128)} %table_hbm.1, f32[2,2,128,768]{3,2,1,0:T(8,128)} %constant.10.clone.spread_hbm, f32[2,2,768,128]{3,2,1,0:T(8,128)} %constant.11.clone.gather_hbm, f32[4,48,8]{2,1,0:T(8,128)} %constant.12.clone.expand_hbm, ...), custom_call_target="tpu_custom_call" | custom-call | tf_op jit(solution)/shard_map/pallas_call | solution.py:504
  35.9 1.9 %copy.10 = f32[32,32,128]{2,1,0:T(8,128)} copy(f32[32,32,128]{2,1,0:T(8,128)} %shard_map.82) | data formatting | bytes 1048576
